TPU v7x, 128 devices: a whole 4x4x4 slice. The times are simulated.
128 devices in a mesh: expert: 16 (over x, y_hi, core), dp: 8 (over y_lo, z).
Axes of the slice: x: 4, y: 4 (y_hi: 2, y_lo: 2; y = y_hi * 2 + y_lo), z: 4, core: 2. Of those that a mesh axis runs over, the one named last changes fastest.
Arguments:
- attn_rows: bfloat16 [16384, 7168], P('dp', 'expert'), may hold values from -6 to 6
- out_grad: bfloat16 [16384, 7168], P('dp', 'expert'), may hold values from -6 to 6
- routes: int32 [16384, 8], P(('dp', 'expert')), may hold values from 0 to 255, as said below
- gates: bfloat16 [16384, 8], P(('dp', 'expert')), may hold values from 0.049804688 to 0.5
- w_gate: bfloat16 [16, 7168, 2048], P('expert', None, 'dp'), may hold values from -0.0625 to 0.0625
- w_up: bfloat16 [16, 7168, 2048], P('expert', None, 'dp'), may hold values from -0.0625 to 0.0625
- w_down: bfloat16 [16, 2048, 7168], P('expert', 'dp'), may hold values from -0.125 to 0.125
Outputs:
- grad_input: bfloat16 [16384, 7168], P('dp', 'expert')
- grad_w_gate: bfloat16 [16, 7168, 2048], P('expert', None, 'dp')
- grad_w_up: bfloat16 [16, 7168, 2048], P('expert', None, 'dp')
Inputs may be any that keep to these rules, and one draw needn't show every extreme that they name: `routes`: each row names 8 different experts. In the 128 rows of one device (aligned blocks of 128 rows) no window expert (below 16) is named by more than 6 rows; in every device's rows some window expert is named by exactly 6 rows, and one window expert is named by exactly 6 rows of every device.
All inputs are finite; a program needn't handle non-finite values.
Results may differ from a plain program's by a relative error of at most 0.0058.
Values may be sent and summed in bfloat16 or wider, within the bound.
A program may use at most 256 MiB of HBM per device.

v0:
```python
import jax
import jax.numpy as jnp
from jax import lax
from jax.sharding import PartitionSpec as P


def slot_tables(route_blocks, experts, capacity):
    matches = (route_blocks[..., None] == jnp.arange(experts, dtype=jnp.int32)).astype(jnp.int32)
    per_token = jnp.sum(matches, axis=2)
    before = jnp.cumsum(per_token, axis=1) - per_token
    slot_of = jnp.sum(matches * before[:, :, None, :], axis=3)
    at_slot = (slot_of[..., None] == jnp.arange(capacity, dtype=jnp.int32)).astype(jnp.float32)
    return (matches.astype(jnp.float32), at_slot)


def deliver(payload, grad_payload, gate_slots, experts, groups):

    def spread(values):
        widened = jnp.broadcast_to(values[:, None], (values.shape[0], groups) + values.shape[1:])
        return widened.reshape((values.shape[0] * groups,) + values.shape[1:])

    arrived = (
        lax.all_to_all(spread(payload), ("expert", "dp"), split_axis=0, concat_axis=0, tiled=True),
        lax.all_to_all(
            spread(grad_payload), ("expert", "dp"), split_axis=0, concat_axis=0, tiled=True
        ),
        lax.all_to_all(
            spread(gate_slots), ("expert", "dp"), split_axis=0, concat_axis=0, tiled=True
        ),
    )

    def regroup(values):
        values = values.reshape((experts, groups) + values.shape[1:])
        return jnp.swapaxes(values, 0, 1)

    return (regroup(arrived[0]), regroup(arrived[1]), regroup(arrived[2]))


def give_back(partial_value, experts, groups):
    outgoing = jnp.swapaxes(partial_value, 0, 1).astype(jnp.bfloat16)
    outgoing = outgoing.reshape((experts * groups,) + partial_value.shape[2:])
    arrived = lax.all_to_all(outgoing, ("expert", "dp"), split_axis=0, concat_axis=0, tiled=True)
    arrived = arrived.reshape((experts, groups) + partial_value.shape[2:]).astype(jnp.float32)
    return jnp.sum(arrived, axis=1)


def expert_pass(token_rows, grad_rows, gate_rows, w_gate, w_up, w_down):
    gate_mat = w_gate[0]
    up_mat = w_up[0]
    down_mat = w_down[0]
    rows_dims = (((1,), (1,)), ((), ()))
    first_dims = (((0,), (0,)), ((), ()))
    gate_pre = jnp.dot(token_rows, gate_mat, preferred_element_type=jnp.float32)
    up_proj = jnp.dot(token_rows, up_mat, preferred_element_type=jnp.float32)
    sigma_gate = jax.nn.sigmoid(gate_pre)
    activated = gate_pre * sigma_gate
    back_proj = lax.dot_general(grad_rows, down_mat, rows_dims, preferred_element_type=jnp.float32)
    coef = gate_rows.astype(jnp.float32)[:, None]
    grad_hidden = coef * back_proj
    grad_gate = (grad_hidden * up_proj * sigma_gate * (1.0 + gate_pre * (1.0 - sigma_gate))).astype(
        jnp.bfloat16
    )
    grad_up = (grad_hidden * activated).astype(jnp.bfloat16)
    g_gate = lax.dot_general(
        token_rows, grad_gate, first_dims, preferred_element_type=jnp.float32
    ).astype(jnp.bfloat16)
    g_up = lax.dot_general(
        token_rows, grad_up, first_dims, preferred_element_type=jnp.float32
    ).astype(jnp.bfloat16)
    partial_value = lax.dot_general(
        grad_gate, gate_mat, rows_dims, preferred_element_type=jnp.float32
    )
    partial_value = partial_value + lax.dot_general(
        grad_up, up_mat, rows_dims, preferred_element_type=jnp.float32
    )
    return (partial_value, g_gate[None], g_up[None])


def per_device(attn_rows, out_grad, routes, gates, w_gate, w_up, w_down):
    experts = lax.axis_size("expert")
    groups = lax.axis_size("dp")
    own_rows = routes.shape[0]
    capacity = 3 * own_rows // 64
    highest = lax.Precision.HIGHEST
    own_matches, own_slots = slot_tables(routes[None], experts, capacity)
    gate_slots = jnp.einsum(
        "btke,btkc,btk->bec",
        own_matches,
        own_slots,
        gates[None].astype(jnp.float32),
        precision=highest,
    )[0].astype(jnp.bfloat16)
    token_rows, grad_rows = (
        lax.all_to_all(attn_rows, "expert", split_axis=0, concat_axis=1, tiled=True),
        lax.all_to_all(out_grad, "expert", split_axis=0, concat_axis=1, tiled=True),
    )
    placement = jnp.einsum("btke,btkc->bect", own_matches, own_slots, precision=highest)[0]
    place_bf = placement.astype(jnp.bfloat16)
    payload = jnp.einsum(
        "ect,td->ecd", place_bf, token_rows, preferred_element_type=jnp.float32
    ).astype(jnp.bfloat16)
    grad_payload = jnp.einsum(
        "ect,td->ecd", place_bf, grad_rows, preferred_element_type=jnp.float32
    ).astype(jnp.bfloat16)
    arrived_x, arrived_dy, arrived_g = deliver(payload, grad_payload, gate_slots, experts, groups)
    width = arrived_x.shape[-1]
    partial_value, g_gate, g_up = expert_pass(
        arrived_x.reshape(-1, width),
        arrived_dy.reshape(-1, width),
        arrived_g.reshape(-1),
        w_gate,
        w_up,
        w_down,
    )
    summed = give_back(partial_value.reshape(arrived_x.shape), experts, groups)
    combined = jnp.einsum("ect,ecd->td", placement, summed, precision=highest).astype(jnp.bfloat16)
    grad_input = lax.all_to_all(combined, "expert", split_axis=1, concat_axis=0, tiled=True)
    return (grad_input, g_gate, g_up)


def solution(mesh):
    return jax.shard_map(
        per_device,
        mesh=mesh,
        in_specs=(
            P("dp", "expert"),
            P("dp", "expert"),
            P(("dp", "expert"), None),
            P(("dp", "expert"), None),
            P("expert", None, "dp"),
            P("expert", None, "dp"),
            P("expert", "dp", None),
        ),
        out_specs=(P("dp", "expert"), P("expert", None, "dp"), P("expert", None, "dp")),
        check_vma=False,
    )
```

profile of v0, /device:TPU:1, one launch (start us, length us, event | category | flops | bytes accessed | tf_op | source)
XLA Modules:
  0.0 850.6 jit_solution(15594823265562110400)
XLA Ops:
  5.1 11.5 %all-to-all-start = ((bf16[128,1,6]{2,1,0:T(2,128)(2,1)}), bf16[128,1,6]{2,1,0:T(2,128)(2,1)S(1)}, u32[]{:S(2)}, u32[]{:S(2)}) async-start(bf16[128,1,6]{2,1,0:T(2,128)(2,1)} %copy.145), calls=%async_computation | async-start | bytes 131072 | tf_op jit(solution)/shard_map/all_to_all | solution.py:27
  18.3 8.1 all-to-all-done
  26.4 4.0 all-to-all-start.1
  30.4 3.2 copy_bitcast_fusion.2
  33.6 22.4 %all-to-all-done.1 = bf16[16,128,448]{1,2,0:T(8,128)(2,1)S(1)} async-done(((bf16[16,128,448]{1,2,0:T(8,128)(2,1)}), bf16[16,128,448]{1,2,0:T(8,128)(2,1)S(1)}, u32[]{:S(2)}, u32[]{:S(2)}) %all-to-all-start.1) | async-done | bytes 1835040 | tf_op jit(solution)/shard_map/all_to_all | solution.py:95
  57.2 5.1 all-to-all-start.3
  67.9 20.0 %all-to-all-done.3 = bf16[16,128,448]{1,2,0:T(8,128)(2,1)S(1)} async-done(((bf16[16,128,448]{1,2,0:T(8,128)(2,1)}), bf16[16,128,448]{1,2,0:T(8,128)(2,1)S(1)}, u32[]{:S(2)}, u32[]{:S(2)}) %all-to-all-start.3) | async-done | bytes 1835040 | tf_op jit(solution)/shard_map/all_to_all | solution.py:94
  87.8 6.4 broadcast_in_dim.11
  94.3 5.9 all-to-all-start.2
  101.7 190.6 %all-to-all-done.2 = bf16[128,6,7168]{2,1,0:T(8,128)(2,1)} async-done(((bf16[128,6,7168]{2,1,0:T(8,128)(2,1)}), bf16[128,6,7168]{2,1,0:T(8,128)(2,1)}, u32[]{:S(2)}, u32[]{:S(2)}) %all-to-all-start.2) | async-done | bytes 11010080 | tf_op jit(solution)/shard_map/all_to_all | solution.py:24
  292.3 5.5 broadcast_in_dim.12
  297.8 12.0 %all-to-all-start.4 = ((bf16[128,6,7168]{2,1,0:T(8,128)(2,1)}), bf16[128,6,7168]{2,1,0:T(8,128)(2,1)}, u32[]{:S(2)}, u32[]{:S(2)}) async-start(bf16[128,6,7168]{2,1,0:T(8,128)(2,1)} %bitcast.110), calls=%async_computation.4 | async-start | bytes 29360128 | tf_op jit(solution)/shard_map/all_to_all | solution.py:23
  310.4 13.5 %copy.153 = bf16[8,16,6,7168]{3,2,1,0:T(8,128)(2,1)} copy(bf16[8,16,6,7168]{3,2,0,1:T(8,128)(2,1)} %bitcast.13) | data formatting | bytes 22020096 | tf_op jit(solution)/shard_map/transpose | solution.py:34
  323.8 16.4 %reshape.122 = bf16[768,7168]{1,0:T(8,128)(2,1)} reshape(bf16[8,16,6,7168]{3,2,1,0:T(8,128)(2,1)} %copy.153) | data formatting | bytes 22020096 | tf_op jit(solution)/shard_map/reshape | solution.py:109
  340.2 157.3 %all-to-all-done.4 = bf16[128,6,7168]{2,1,0:T(8,128)(2,1)} async-done(((bf16[128,6,7168]{2,1,0:T(8,128)(2,1)}), bf16[128,6,7168]{2,1,0:T(8,128)(2,1)}, u32[]{:S(2)}, u32[]{:S(2)}) %all-to-all-start.4) | async-done | bytes 11010080 | tf_op jit(solution)/shard_map/all_to_all | solution.py:23
  497.5 13.5 %copy.159 = bf16[8,16,6,7168]{3,2,1,0:T(8,128)(2,1)} copy(bf16[8,16,6,7168]{3,2,0,1:T(8,128)(2,1)} %bitcast.21) | data formatting | bytes 22020096 | tf_op jit(solution)/shard_map/transpose | solution.py:34
  511.0 15.5 %reshape.125 = bf16[768,7168]{1,0:T(8,128)(2,1)} reshape(bf16[8,16,6,7168]{3,2,1,0:T(8,128)(2,1)} %copy.159) | data formatting | bytes 22020096 | tf_op jit(solution)/shard_map/reshape | solution.py:108
  526.6 7.0 fusion.5
  533.6 6.7 multiply_convert_fusion
  540.5 3.1 fusion.25
  543.6 9.1 %fusion.3 = f32[768,7168]{1,0:T(8,128)} fusion(bf16[768,256]{1,0:T(8,128)(2,1)S(1)} %fusion.25, bf16[1,7168,256]{2,1,0:T(8,128)(2,1)S(1)} %copy-done.4), kind=kOutput, calls=%fused_computation.11 | convolution fusion | flops 2818572288 | bytes 26083328 | tf_op jit(solution)/shard_map/dot_general | solution.py:70
  552.7 13.2 %add_convert_fusion = bf16[768,7168]{1,0:T(8,128)(2,1)} fusion(f32[768,7168]{1,0:T(8,128)} %fusion.3, bf16[768,256]{1,0:T(8,128)(2,1)S(1)} %get-tuple-element.3, bf16[1,7168,256]{2,1,0:T(8,128)(2,1)} %param.12), kind=kOutput, calls=%fused_computation.1 | convolution fusion | flops 2829582336 | bytes 37093376 | tf_op jit(solution)/shard_map/dot_general | solution.py:73
  565.9 15.9 %convert_element_type.104 = bf16[8,16,6,7168]{3,2,1,0:T(8,128)(2,1)} reshape(bf16[768,7168]{1,0:T(8,128)(2,1)} %add_convert_fusion) | data formatting | bytes 22020096 | tf_op jit(solution)/shard_map/convert_element_type | solution.py:40
  581.8 11.0 %copy.183 = bf16[16,8,6,7168]{3,1,0,2:T(8,128)(2,1)S(1)} copy(bf16[16,8,6,7168]{3,2,0,1:T(8,128)(2,1)} %bitcast.109) | data formatting | bytes 22020096 | tf_op jit(solution)/shard_map/convert_element_type | solution.py:40
  592.9 30.0 %copy.161 = bf16[128,6,7168]{2,1,0:T(8,128)(2,1)S(1)} copy(bf16[128,6,7168]{2,0,1:T(8,128)(2,1)S(1)} %bitcast.112) | data formatting | bytes 22020096 | tf_op jit(solution)/shard_map/reshape | solution.py:41
  622.9 179.2 %all_to_all.81 = bf16[128,6,7168]{2,1,0:T(8,128)(2,1)S(1)} all-to-all(bf16[128,6,7168]{2,1,0:T(8,128)(2,1)S(1)} %copy.161), channel_id=1, replica_groups=mesh['expert'=16,'dp'=8] {'expert','dp'}, dimensions={0} | all-to-all | bytes 22020096 | tf_op jit(solution)/shard_map/all_to_all | solution.py:42
  802.1 4.1 convert_reduce_fusion
  806.2 7.6 fusion.2
  816.1 5.9 all-to-all-start.6
  822.0 9.1 %fusion = bf16[1,7168,256]{2,1,0:T(8,128)(2,1)} fusion(bf16[768,7168]{1,0:T(8,128)(2,1)} %reshape.125, bf16[768,256]{1,0:T(8,128)(2,1)S(1)} %fusion.25), kind=kOutput, calls=%fused_computation.5 | convolution fusion | flops 2820407296 | bytes 15073280 | tf_op jit(solution)/shard_map/dot_general | solution.py:64
  831.1 9.2 %fusion.1 = bf16[1,7168,256]{2,1,0:T(8,128)(2,1)} fusion(bf16[768,7168]{1,0:T(8,128)(2,1)} %reshape.125, bf16[768,256]{1,0:T(8,128)(2,1)S(1)} %get-tuple-element.3), kind=kOutput, calls=%fused_computation.6 | convolution fusion | flops 2820407296 | bytes 15073280 | tf_op jit(solution)/shard_map/dot_general | solution.py:67
  840.2 7.4 all-to-all-done.6
  (51 shorter events, 20.3 us)
Async XLA Ops:
  0.6 15.9 %copy-start = (bf16[2048,448]{0,1:T(8,128)(2,1)S(1)}, bf16[2048,448]{0,1:T(8,128)(2,1)}, u32[]{:S(2)}) copy-start(bf16[2048,448]{0,1:T(8,128)(2,1)} %param.8) | copy-start | bytes 5505028
  5.1 21.3 %all-to-all-start = ((bf16[128,1,6]{2,1,0:T(2,128)(2,1)}), bf16[128,1,6]{2,1,0:T(2,128)(2,1)S(1)}, u32[]{:S(2)}, u32[]{:S(2)}) async-start(bf16[128,1,6]{2,1,0:T(2,128)(2,1)} %copy.145), calls=%async_computation | async-start | bytes 131072 | tf_op jit(solution)/shard_map/all_to_all | solution.py:27
  26.4 29.6 %all-to-all-start.1 = ((bf16[16,128,448]{1,2,0:T(8,128)(2,1)}), bf16[16,128,448]{1,2,0:T(8,128)(2,1)S(1)}, u32[]{:S(2)}, u32[]{:S(2)}) async-start(bf16[16,128,448]{1,2,0:T(8,128)(2,1)} %copy_bitcast_fusion.3), calls=%async_computation.1 | async-start | bytes 3670016 | tf_op jit(solution)/shard_map/all_to_all | solution.py:95
  30.4 32.2 %copy-start.5 = (s32[128,8]{0,1:T(8,128)S(1)}, s32[128,8]{0,1:T(8,128)}, u32[]{:S(2)}) copy-start(s32[128,8]{0,1:T(8,128)} %param.9) | copy-start | bytes 12292
  56.0 1.2 copy-start.2
  57.2 30.6 %all-to-all-start.3 = ((bf16[16,128,448]{1,2,0:T(8,128)(2,1)}), bf16[16,128,448]{1,2,0:T(8,128)(2,1)S(1)}, u32[]{:S(2)}, u32[]{:S(2)}) async-start(bf16[16,128,448]{1,2,0:T(8,128)(2,1)} %copy_bitcast_fusion.2), calls=%async_computation.3 | async-start | bytes 3670016 | tf_op jit(solution)/shard_map/all_to_all | solution.py:94
  94.3 198.0 %all-to-all-start.2 = ((bf16[128,6,7168]{2,1,0:T(8,128)(2,1)}), bf16[128,6,7168]{2,1,0:T(8,128)(2,1)}, u32[]{:S(2)}, u32[]{:S(2)}) async-start(bf16[128,6,7168]{2,1,0:T(8,128)(2,1)} %bitcast.111), calls=%async_computation.2 | async-start | bytes 29360128 | tf_op jit(solution)/shard_map/all_to_all | solution.py:24
  297.8 199.8 %all-to-all-start.4 = ((bf16[128,6,7168]{2,1,0:T(8,128)(2,1)}), bf16[128,6,7168]{2,1,0:T(8,128)(2,1)}, u32[]{:S(2)}, u32[]{:S(2)}) async-start(bf16[128,6,7168]{2,1,0:T(8,128)(2,1)} %bitcast.110), calls=%async_computation.4 | async-start | bytes 29360128 | tf_op jit(solution)/shard_map/all_to_all | solution.py:23
  526.6 7.0 copy-start.6
  526.6 13.8 %slice-start = ((s8[11010048]{0:T(1024)(128)(4,1)}), s8[4194304]{0:T(1024)(128)(4,1)S(1)}, s32[]{:S(2)}) async-start(s8[11010048]{0:T(1024)(128)(4,1)} %bitcast.113), calls=%async_computation.7 | async-start | bytes 8388608
  526.6 13.8 %slice-start.1 = ((s8[11010048]{0:T(1024)(128)(4,1)}), s8[4194304]{0:T(1024)(128)(4,1)S(1)}, s32[]{:S(2)}) async-start(s8[11010048]{0:T(1024)(128)(4,1)} %bitcast.113), calls=%async_computation.8 | async-start | bytes 8388608
  533.6 6.8 slice-start.2
  533.6 6.9 copy-start.3
  540.5 3.1 copy-start.4
  816.1 31.5 %all-to-all-start.6 = ((bf16[128,16,448]{0,2,1:T(8,128)(2,1)}), bf16[128,16,448]{0,2,1:T(8,128)(2,1)}, u32[]{:S(2)}, u32[]{:S(2)}) async-start(bf16[128,16,448]{0,2,1:T(8,128)(2,1)} %bitcast.28), calls=%async_computation.6 | async-start | bytes 3670016 | tf_op jit(solution)/shard_map/all_to_all | solution.py:117
  831.1 19.5 %copy-start.1 = (bf16[2048,448]{0,1:T(8,128)(2,1)S(1)}, bf16[2048,448]{0,1:T(8,128)(2,1)}, u32[]{:S(2)}) copy-start(bf16[2048,448]{0,1:T(8,128)(2,1)} %param.8) | copy-start | bytes 5505028
where the time goes:
time: 853 us; the launch traced here: 851 us
  waiting for transfers between devices  406 us (48%)
  blocking collectives  179 us (21%)
  local copies, waits for them, and re-layouts  144 us (17%)
  matrix products  69.3 us (8%)
  starting transfers between devices  44.4 us (5%)
    all_to_all x1, waiting for transfers between devices, deliver(): lax.all_to_all(spread(grad_payload), ('expert', 'dp'), split_axis=0, conc...  191 us
    all_to_all x1, blocking collectives, give_back(): lax.all_to_all(outgoing, ('expert', 'dp'), split_axis=0, concat_axis=0, t...  179 us
    all_to_all x1, waiting for transfers between devices, deliver(): lax.all_to_all(spread(payload), ('expert', 'dp'), split_axis=0, concat_ax...  157 us
    reshape x1, local copies, waits for them, and re-layouts, give_back(): outgoing = outgoing.reshape((experts * groups,) + partial_value.shape[2:])  30 us
    transpose x2, local copies, waits for them, and re-layouts, regroup(): return jnp.swapaxes(values, 0, 1)  27 us
    convert_element_type x2, local copies, waits for them, and re-layouts, give_back(): outgoing = jnp.swapaxes(partial_value, 0, 1).astype(jnp.bfloat16)  26.9 us
    all_to_all x1, waiting for transfers between devices, per_device(): lax.all_to_all(out_grad, 'expert', split_axis=0, concat_axis=1, tiled=True)  22.4 us
    all_to_all x1, waiting for transfers between devices, per_device(): lax.all_to_all(attn_rows, 'expert', split_axis=0, concat_axis=1, tiled=True)  20 us
  transfers between devices with their start and end apart: 6, of which 6 were waited for; matrix products, arithmetic and copies ran while one was open for 7% of the time, Pallas kernels for 0%

commit v1 on v0

v1 whole, which is shorter than its diff:
```python
import jax
import jax.numpy as jnp
from jax import lax
from jax.sharding import PartitionSpec as P

BF = jnp.bfloat16
F32 = jnp.float32


def slot_tables(routes, gates, experts, capacity):
    matches = (routes[..., None] == jnp.arange(experts, dtype=routes.dtype)).astype(F32)
    per_token = jnp.sum(matches, axis=2)
    coef = jnp.sum(matches * gates[..., None].astype(F32), axis=2)
    tokens = routes.shape[1]
    earlier = (jnp.arange(tokens)[:, None] < jnp.arange(tokens)[None, :]).astype(BF)
    before = jnp.einsum("bse,st->bte", per_token.astype(BF), earlier, preferred_element_type=F32)
    slot = jnp.arange(capacity, dtype=F32)
    hit = (before[..., None] == slot) & (per_token[..., None] > 0)
    hit = jnp.transpose(hit, (0, 2, 3, 1))
    scaled = jnp.where(hit, jnp.transpose(coef, (0, 2, 1))[:, :, None, :], 0.0)
    return hit.astype(BF), scaled.astype(BF)


def per_device(attn_rows, out_grad, routes, gates, w_gate, w_up, w_down):
    experts = lax.axis_size("expert")
    groups = lax.axis_size("dp")
    own = routes.shape[0]
    capacity = 3 * own // 64
    width = attn_rows.shape[1]
    packed = jnp.concatenate([routes.astype(BF), gates], axis=1)
    packed = lax.all_gather(packed, "expert", axis=0, tiled=False)
    top = routes.shape[1]
    place, scaled = slot_tables(packed[..., :top], packed[..., top:], experts, capacity)

    def dispatch(table, rows):
        rows = rows.reshape(experts, own, width)
        sent = jnp.einsum("bect,btd->ebcd", table, rows, preferred_element_type=F32).astype(BF)
        sent = sent.reshape(experts, experts * capacity, width)
        got = lax.all_to_all(sent, "expert", split_axis=0, concat_axis=0, tiled=True)
        got = jnp.transpose(got, (1, 0, 2)).reshape(experts * capacity, experts * width)
        return lax.all_gather(got, "dp", axis=0, tiled=True)

    x = dispatch(place, attn_rows)
    dy = dispatch(scaled, out_grad)

    gate_mat, up_mat, down_mat = w_gate[0], w_up[0], w_down[0]
    rows_dims = (((1,), (1,)), ((), ()))
    first_dims = (((0,), (0,)), ((), ()))
    g = jnp.dot(x, gate_mat, preferred_element_type=F32)
    u = jnp.dot(x, up_mat, preferred_element_type=F32)
    gh = lax.dot_general(dy, down_mat, rows_dims, preferred_element_type=F32)
    s = jax.nn.sigmoid(g)
    dg = (gh * u * s * (1.0 + g * (1.0 - s))).astype(BF)
    du = (gh * (g * s)).astype(BF)
    part = lax.dot_general(dg, gate_mat, rows_dims, preferred_element_type=F32)
    part = (part + lax.dot_general(du, up_mat, rows_dims, preferred_element_type=F32)).astype(BF)
    back = lax.psum_scatter(part, "dp", scatter_dimension=0, tiled=True)
    g_gate = lax.dot_general(x, dg, first_dims, preferred_element_type=F32).astype(BF)
    g_up = lax.dot_general(x, du, first_dims, preferred_element_type=F32).astype(BF)
    back = back.reshape(experts * capacity, experts, width)
    back = jnp.transpose(back, (1, 0, 2))
    back = lax.all_to_all(back, "expert", split_axis=0, concat_axis=0, tiled=True)
    back = back.reshape(experts, experts, capacity, width)
    grad_input = jnp.einsum("bect,ebcd->btd", place, back, preferred_element_type=F32).astype(BF)
    return grad_input.reshape(experts * own, width), g_gate[None], g_up[None]


def solution(mesh):
    return jax.shard_map(
        per_device,
        mesh=mesh,
        in_specs=(
            P("dp", "expert"),
            P("dp", "expert"),
            P(("dp", "expert"), None),
            P(("dp", "expert"), None),
            P("expert", None, "dp"),
            P("expert", None, "dp"),
            P("expert", "dp", None),
        ),
        out_specs=(P("dp", "expert"), P("expert", None, "dp"), P("expert", None, "dp")),
        check_vma=False,
    )
```

time: 853 us -> 515 us (0.60)
  local copies, waits for them, and re-layouts: 144 us -> 21.8 us
  blocking collectives: 179 us -> 80.2 us
  waiting for transfers between devices: 406 us -> 328 us
  starting transfers between devices: 44.4 us -> 7.45 us
  between operations: 0.91 us -> 13.9 us
    all_to_all x6 -> x1, waiting for transfers between devices: 406 us -> 4.56 us  [per_device(): lax.all_to_all(back, 'expert', split_axis=0, concat_axis=0, tiled=True)]
    all_gather x0 -> x2, waiting for transfers between devices: none -> 207 us  [dispatch(): return lax.all_gather(got, 'dp', axis=0, tiled=True)]
    all_to_all x1 -> x2, blocking collectives: 179 us -> 54.4 us  [dispatch(): lax.all_to_all(sent, 'expert', split_axis=0, concat_axis=0, tiled=True)]
    reduce_scatter x0 -> x1, waiting for transfers between devices: none -> 117 us  [per_device(): back = lax.psum_scatter(part, 'dp', scatter_dimension=0, tiled=True)]
    reshape x3 -> x7, local copies, waits for them, and re-layouts: 61.9 us -> 14 us  [the longest x2 5.37 us: dispatch(): jnp.transpose(got, (1, 0, 2)).reshape(experts * capacity, experts * width)]
    all_to_all x6 -> x1, starting transfers between devices: 44.4 us -> 7.15 us  [per_device(): lax.all_to_all(back, 'expert', split_axis=0, concat_axis=0, tiled=True)]
    convert_element_type x10 -> x0, local copies, waits for them, and re-layouts: 32.8 us -> none  [the longest x2 26.9 us: give_back(): outgoing = jnp.swapaxes(partial_value, 0, 1).astype(jnp.bfloat16)]
    all_gather x0 -> x1, blocking collectives: none -> 25.8 us  [per_device(): packed = lax.all_gather(packed, 'expert', axis=0, tiled=False)]
  transfers between devices with their start and end apart: 6 -> 4, of which waited for: 6 -> 4; matrix products, arithmetic and copies ran while one was open for 7% -> 6% of each run, Pallas kernels for 0% -> 0%
where the time goes in v1:
time: 515 us; the launch traced here: 514 us
  waiting for transfers between devices  328 us (64%)
  blocking collectives  80.2 us (16%)
  matrix products  60.9 us (12%)
  local copies, waits for them, and re-layouts  21.8 us (4%)
  between operations  13.9 us (3%)
  starting transfers between devices  7.45 us (1%)
    all_gather x2, waiting for transfers between devices, dispatch(): return lax.all_gather(got, 'dp', axis=0, tiled=True)  207 us
    reduce_scatter x1, waiting for transfers between devices, per_device(): back = lax.psum_scatter(part, 'dp', scatter_dimension=0, tiled=True)  117 us
    all_to_all x2, blocking collectives, dispatch(): lax.all_to_all(sent, 'expert', split_axis=0, concat_axis=0, tiled=True)  54.4 us
    all_gather x1, blocking collectives, per_device(): packed = lax.all_gather(packed, 'expert', axis=0, tiled=False)  25.8 us
    dot_general x1, matrix products, per_device(): lax.dot_general(du, up_mat, rows_dims, preferred_element_type=F32)  12.6 us
  transfers between devices with their start and end apart: 4, of which 4 were waited for; matrix products, arithmetic and copies ran while one was open for 6% of the time, Pallas kernels for 0%

profile of v1, /device:TPU:1, one launch (start us, length us, event | category | flops | bytes accessed | tf_op | source)
XLA Modules:
  0.0 514.2 jit_solution(15024579949341409885)
XLA Ops:
  7.2 0.7 convert_element_type.48
  8.6 25.8 %all-gather = bf16[2048,16]{0,1:T(8,128)(2,1)S(1)} all-gather(bf16[128,16]{0,1:T(8,128)(2,1)S(1)} %pad_maximum_fusion), channel_id=2, replica_groups=mesh['expert'=16,'dp'=8] {'expert'}, dimensions={0}, use_global_device_ids=true | all-gather | bytes 69632 | tf_op jit(solution)/shard_map/all_gather | solution.py:31
  34.4 0.8 convert_reduce_fusion
  35.5 2.0 copy.62
  37.5 0.9 fusion.18
  38.4 0.9 copy.45
  39.3 25.1 %all_to_all.15 = bf16[16,96,448]{2,1,0:T(8,128)(2,1)S(1)} all-to-all(bf16[16,96,448]{2,1,0:T(8,128)(2,1)S(1)} %copy.45), channel_id=1, replica_groups=mesh['expert'=16,'dp'=8] {'expert'}, dimensions={0} | all-to-all | bytes 2752512 | tf_op jit(solution)/shard_map/all_to_all | solution.py:39
  64.4 0.9 copy.46
  65.3 2.7 reshape.47
  68.8 0.9 fusion.15
  69.7 0.9 copy.42
  70.6 29.3 %all_to_all.16 = bf16[16,96,448]{2,1,0:T(8,128)(2,1)S(1)} all-to-all(bf16[16,96,448]{2,1,0:T(8,128)(2,1)S(1)} %copy.42), channel_id=1, replica_groups=mesh['expert'=16,'dp'=8] {'expert'}, dimensions={0} | all-to-all | bytes 2752512 | tf_op jit(solution)/shard_map/all_to_all | solution.py:39
  99.9 0.9 copy.43
  100.8 2.7 reshape.44
  103.7 96.4 %all-gather.6.cloned.1.call-done = bf16[768,7168]{1,0:T(8,128)(2,1)} async-done(((bf16[96,7168]{1,0:T(8,128)(2,1)}), bf16[768,7168]{1,0:T(8,128)(2,1)}) %all-gather.6.cloned.1.call-update) | async-done | bytes 11010064 | tf_op jit(solution)/shard_map/all_gather | solution.py:41
  200.1 6.9 %fusion.4 = f32[768,256]{1,0:T(8,128)S(1)} fusion(bf16[768,7168]{1,0:T(8,128)(2,1)} %all-gather.6.cloned.1.call-done, bf16[1,7168,256]{2,1,0:T(8,128)(2,1)} %param.11), kind=kOutput, calls=%fused_computation.8 | convolution fusion | flops 2818572288 | bytes 15466496 | tf_op jit(solution)/shard_map/dot_general | solution.py:49
  207.0 110.1 %all-gather.4.cloned.1.call-done = bf16[768,7168]{1,0:T(8,128)(2,1)} async-done(((bf16[96,7168]{1,0:T(8,128)(2,1)}), bf16[768,7168]{1,0:T(8,128)(2,1)}) %all-gather.4.cloned.1.call-update) | async-done | bytes 11010064 | tf_op jit(solution)/shard_map/all_gather | solution.py:41
  317.2 7.1 %multiply_convert_fusion = (bf16[768,256]{1,0:T(8,128)(2,1)S(1)}, f32[768,256]{1,0:T(8,128)S(1)}) fusion(f32[768,256]{1,0:T(8,128)S(1)} %fusion.4, bf16[768,7168]{1,0:T(8,128)(2,1)} %all-gather.4.cloned.1.call-done, bf16[1,256,7168]{2,1,0:T(8,128)(2,1)} %param.13), kind=kOutput, calls=%fused_computation.30 | convolution fusion | flops 2819751936 | bytes 16646144 | tf_op jit(solution)/shard_map/dot_general | solution.py:51
  324.3 2.4 copy-done.6
  326.6 4.5 fusion.31
  331.1 9.1 %fusion.2 = f32[768,7168]{1,0:T(8,128)} fusion(bf16[768,256]{1,0:T(8,128)(2,1)S(1)} %fusion.31, bf16[1,7168,256]{2,1,0:T(8,128)(2,1)S(1)} %copy-done.1), kind=kOutput, calls=%fused_computation.6 | convolution fusion | flops 2818572288 | bytes 26083328 | tf_op jit(solution)/shard_map/dot_general | solution.py:55
  340.2 12.6 %add_convert_fusion = bf16[768,7168]{1,0:T(8,128)(2,1)} fusion(f32[768,7168]{1,0:T(8,128)} %fusion.2, bf16[768,256]{1,0:T(8,128)(2,1)S(1)} %get-tuple-element.7, bf16[1,7168,256]{2,1,0:T(8,128)(2,1)S(1)} %copy-done), kind=kOutput, calls=%fused_computation | convolution fusion | flops 2829582336 | bytes 37093376 | tf_op jit(solution)/shard_map/dot_general | solution.py:56
  352.8 116.6 %reduce-scatter.2.cloned.1.call-done = bf16[96,7168]{1,0:T(8,128)(2,1)} async-done(((bf16[768,7168]{1,0:T(8,128)(2,1)}), bf16[96,7168]{1,0:T(8,128)(2,1)}) %reduce-scatter.2.cloned.1.call-update) | async-done | bytes 1376272 | tf_op jit(solution)/shard_map/reduce_scatter | solution.py:57
  469.3 3.1 reshape.48
  472.5 2.0 copy.75
  474.5 7.1 %all-to-all-start.2 = ((bf16[16,96,448]{2,1,0:T(8,128)(2,1)}), bf16[16,96,448]{2,1,0:T(8,128)(2,1)S(1)}, u32[]{:S(2)}, u32[]{:S(2)}) async-start(bf16[16,96,448]{2,1,0:T(8,128)(2,1)} %bitcast.80), calls=%async_computation.3 | async-start | bytes 3145728 | tf_op jit(solution)/shard_map/all_to_all | solution.py:62
  481.6 9.1 %fusion = bf16[1,7168,256]{2,1,0:T(8,128)(2,1)} fusion(bf16[768,7168]{1,0:T(8,128)(2,1)} %all-gather.6.cloned.1.call-done, bf16[768,256]{1,0:T(8,128)(2,1)S(1)} %fusion.31), kind=kOutput, calls=%fused_computation.3 | convolution fusion | flops 2820407296 | bytes 15073280 | tf_op jit(solution)/shard_map/dot_general | solution.py:58
  490.7 9.1 %fusion.1 = bf16[1,7168,256]{2,1,0:T(8,128)(2,1)} fusion(bf16[768,7168]{1,0:T(8,128)(2,1)} %all-gather.6.cloned.1.call-done, bf16[768,256]{1,0:T(8,128)(2,1)S(1)} %get-tuple-element.7), kind=kOutput, calls=%fused_computation.4 | convolution fusion | flops 2820407296 | bytes 15073280 | tf_op jit(solution)/shard_map/dot_general | solution.py:59
  499.8 4.6 all-to-all-done.2
  504.3 0.9 copy.48
  505.2 0.8 fusion.21
  506.0 1.7 copy.74
  (29 shorter events, 2.0 us)
Async XLA Ops:
  7.2 193.0 %all-gather.6.cloned.1.call-start = ((), (), s32[]{:S(2)}) async-start(), calls=%async_computation.5 | async-start | bytes 12386304 | tf_op jit(solution)/shard_map/all_gather | solution.py:41
  35.3 3.1 copy-start.3
  64.4 3.6 copy-start.2
  68.0 0.8 copy-start.4
  68.0 0.9 copy-start.5
  68.0 249.2 %all-gather.4.cloned.1.call-start = ((), (), s32[]{:S(2)}) async-start(), calls=%async_computation.4 | async-start | bytes 12386304 | tf_op jit(solution)/shard_map/all_gather | solution.py:41
  103.5 365.8 %reduce-scatter.2.cloned.1.call-start = ((), (), s32[]{:S(2)}) async-start(), calls=%async_computation.6 | async-start | bytes 12386304 | tf_op jit(solution)/shard_map/reduce_scatter | solution.py:57
  207.0 117.3 %copy-start.7 = (f32[768,256]{1,0:T(8,128)}, f32[768,256]{1,0:T(8,128)S(1)}, u32[]{:S(2)}) copy-start(f32[768,256]{1,0:T(8,128)S(1)} %fusion.4) | copy-start | bytes 2359300
  317.2 7.1 %copy-start = (bf16[1,7168,256]{2,1,0:T(8,128)(2,1)S(1)}, bf16[1,7168,256]{2,1,0:T(8,128)(2,1)}, u32[]{:S(2)}) copy-start(bf16[1,7168,256]{2,1,0:T(8,128)(2,1)} %param.12) | copy-start | bytes 11010052
  317.2 9.5 %copy-start.6 = (bf16[768,7168]{1,0:T(8,128)(2,1)S(1)}, bf16[768,7168]{1,0:T(8,128)(2,1)}, u32[]{:S(2)}) copy-start(bf16[768,7168]{1,0:T(8,128)(2,1)} %all-gather.6.cloned.1.call-done) | copy-start | bytes 33030148
  326.6 4.5 copy-start.1
  474.5 29.8 %all-to-all-start.2 = ((bf16[16,96,448]{2,1,0:T(8,128)(2,1)}), bf16[16,96,448]{2,1,0:T(8,128)(2,1)S(1)}, u32[]{:S(2)}, u32[]{:S(2)}) async-start(bf16[16,96,448]{2,1,0:T(8,128)(2,1)} %bitcast.80), calls=%async_computation.3 | async-start | bytes 3145728 | tf_op jit(solution)/shard_map/all_to_all | solution.py:62
Sparse Core Ops, SparseCore 0:
  68.1 131.9 all-gather.5
  202.3 114.7 all-gather.3
  352.9 116.4 reduce-scatter.1

commit v2 on v1

v2 whole, which is shorter than its diff:
```python
import functools

import jax
import jax.numpy as jnp
from jax import lax
from jax.experimental import pallas as pl
from jax.experimental.pallas import tpu as pltpu
from jax.sharding import PartitionSpec as P

BF = jnp.bfloat16
F32 = jnp.float32
MESH = pl.DeviceIdType.MESH
NT = (((1,), (1,)), ((), ()))
EXP, DP, NZ, CHIPS = 16, 8, 4, 8
TOK, TOP, CAP = 128, 8, 6
LOCAL = EXP * TOK
WIDE, D, HID = 896, 7168, 256
PIECE = 48
SHARD = 96
STEP = 1024


def gather_kernel(
    xt_ref, dt_ref, pk_ref, wg_ref, wu_ref, wd_ref,
    x_out, dg_ref, du_ref,
    raw, tabs, code, coef, onehot, pay, xall, dall, wg, wu, wd, acc,
    ssem, rsem, lsem,
):
    ex = lax.axis_index("expert")
    dp = lax.axis_index("dp")
    core = ex % 2
    chip = ex // 2
    row, z = dp // NZ, dp % NZ

    def at(dy, dz):
        return (row + dy) % 2 * NZ + (z + dz) % NZ

    up, down, side = at(0, 1), at(0, NZ - 1), at(1, 0)
    bufs = (xall, dall)

    barrier = pltpu.get_barrier_semaphore()
    for r in range(1, EXP):
        pl.semaphore_signal(barrier, inc=1, device_id=((ex + r) % EXP, dp), device_id_type=MESH)
    for peer in (up, down, side):
        pl.semaphore_signal(barrier, inc=1, device_id=(ex, peer), device_id_type=MESH)

    local = []

    def copy_in(src, dst):
        c = pltpu.make_async_copy(src, dst, lsem.at[len(local)])
        c.start()
        local.append(c)
        return c

    mine = pl.ds(pl.multiple_of(core * (WIDE // 2), WIDE // 2), WIDE // 2)
    lanes = pl.ds(pl.multiple_of(ex * TOK, TOK), TOK)
    in_tab = copy_in(pk_ref, tabs.at[:, lanes])
    in_raw = [copy_in(ref, raw.at[t, mine, :]) for t, ref in enumerate((xt_ref, dt_ref))]
    in_w = [copy_in(wg_ref, wg), copy_in(wu_ref, wu), copy_in(wd_ref, wd)]

    pl.semaphore_wait(barrier, EXP - 1 + 3)

    sent = []
    slots = [0]

    def slot():
        slots[0] += 1
        return slots[0] - 1

    def send(k, src, dst, device):
        c = pltpu.make_async_remote_copy(
            src_ref=src, dst_ref=dst, send_sem=ssem.at[k], recv_sem=rsem.at[k],
            device_id=device, device_id_type=MESH,
        )
        c.start()
        sent.append(c)

    def arrive(k, dst):
        pltpu.make_async_remote_copy(
            src_ref=dst, dst_ref=dst, send_sem=ssem.at[k], recv_sem=rsem.at[k],
            device_id=(ex, side), device_id_type=MESH,
        ).wait_recv()

    other = pl.ds(pl.multiple_of((1 - core) * (WIDE // 2), WIDE // 2), WIDE // 2)
    tab_slot = [slot() for _ in range(EXP)]
    for r in range(1, EXP):
        send(tab_slot[r], pk_ref, tabs.at[:, lanes], ((ex + r) % EXP, dp))
    raw_slot = [slot(), slot()]
    sibling = (chip * 2 + 1 - core, dp)
    for t, ref in enumerate((xt_ref, dt_ref)):
        send(raw_slot[t], ref, raw.at[t, mine, :], sibling)

    in_tab.wait()
    for r in range(1, EXP):
        src = (ex + EXP - r) % EXP
        arrive(tab_slot[r], tabs.at[:, pl.ds(pl.multiple_of(src * TOK, TOK), TOK)])

    table = tabs[...].astype(F32)
    route, gate = table[:TOP], table[TOP:]
    ids = (lax.broadcasted_iota(jnp.int32, (CHIPS, LOCAL), 0) * 2 + core).astype(F32)
    hit = jnp.zeros((CHIPS, LOCAL), F32)
    weight = jnp.zeros((CHIPS, LOCAL), F32)
    for k in range(TOP):
        same = route[k : k + 1] == ids
        hit = hit + jnp.where(same, 1.0, 0.0)
        weight = weight + jnp.where(same, gate[k : k + 1], 0.0)
    coef[...] = weight
    stacked = jnp.concatenate([hit[:, b * TOK : (b + 1) * TOK] for b in range(EXP)], axis=0)
    tri = (
        lax.broadcasted_iota(jnp.int32, (TOK, TOK), 0) < lax.broadcasted_iota(jnp.int32, (TOK, TOK), 1)
    ).astype(F32).astype(BF)
    before = jnp.dot(stacked.astype(BF), tri, preferred_element_type=F32)
    for b in range(EXP):
        part = slice(b * CHIPS, (b + 1) * CHIPS)
        code[:, b * TOK : (b + 1) * TOK] = jnp.where(
            stacked[part] > 0.0, before[part] + float(CAP * (b % CHIPS)), -1.0
        )

    slot_row = lax.broadcasted_iota(jnp.int32, (PIECE, LOCAL // 2), 0).astype(F32)
    own_rows = [pl.ds(pl.multiple_of(dp * SHARD + h * PIECE, PIECE), PIECE) for h in range(2)]
    chip_cols = pl.ds(pl.multiple_of(chip * WIDE, WIDE), WIDE)
    a2a_slot = [[[slot() for _ in range(CHIPS)] for _ in range(2)] for _ in range(2)]
    a2a_self = [[None, None], [None, None]]

    def dispatch(t, h):
        half = slice(h * (LOCAL // 2), (h + 1) * (LOCAL // 2))
        for i in range(CHIPS):
            equal = code[i : i + 1, half] == slot_row
            value = 1.0 if t == 0 else coef[i : i + 1, half]
            onehot[i * PIECE : (i + 1) * PIECE] = jnp.where(equal, value, 0.0).astype(BF)
        for n in range(0, WIDE, 128):
            got = lax.dot_general(onehot[...], raw[t, n : n + 128, half], NT, preferred_element_type=F32)
            pay[t, h, :, :, n : n + 128] = got.astype(BF).reshape(CHIPS, PIECE, 128)
        where = bufs[t].at[own_rows[h], chip_cols]
        for r in range(1, CHIPS):
            to = (chip + r) % CHIPS
            send(a2a_slot[t][h][r], pay.at[t, h, to], where, (to * 2 + core, dp))
        a2a_self[t][h] = copy_in(pay.at[t, h, chip], where)

    def complete(t, h):
        a2a_self[t][h].wait()
        for r in range(1, CHIPS):
            src = (chip + CHIPS - r) % CHIPS
            arrive(a2a_slot[t][h][r], bufs[t].at[own_rows[h], pl.ds(pl.multiple_of(src * WIDE, WIDE), WIDE)])

    def piece(t, h, s):
        return bufs[t].at[pl.ds(pl.multiple_of(s * SHARD + h * PIECE, PIECE), PIECE), :]

    def slots_for():
        return {(t, h): slot() for t in range(2) for h in range(2)}

    to_up, to_down, to_side = slots_for(), slots_for(), slots_for()

    def spread(t, h):
        for k, peer in ((to_side, side), (to_up, up), (to_down, down)):
            send(k[t, h], piece(t, h, dp), piece(t, h, dp), (ex, peer))

    in_raw[0].wait()
    arrive(raw_slot[0], raw.at[0, other, :])
    dispatch(0, 0)
    dispatch(0, 1)
    complete(0, 0)
    spread(0, 0)
    in_raw[1].wait()
    arrive(raw_slot[1], raw.at[1, other, :])
    dispatch(1, 0)
    complete(0, 1)
    spread(0, 1)
    dispatch(1, 1)
    complete(1, 0)
    spread(1, 0)
    complete(1, 1)
    spread(1, 1)
    for c in in_w:
        c.wait()

    def rows_of(s):
        return pl.ds(pl.multiple_of(s * SHARD, SHARD), SHARD)

    def hidden(s):
        rows = rows_of(s)
        acc[...] = jnp.zeros_like(acc)

        def contract(k, _):
            cols = pl.ds(pl.multiple_of(k * STEP, STEP), STEP)
            xs = xall[rows, cols]
            acc[0] += jnp.dot(xs, wg[cols, :], preferred_element_type=F32)
            acc[1] += jnp.dot(xs, wu[cols, :], preferred_element_type=F32)
            acc[2] += lax.dot_general(dall[rows, cols], wd[:, cols], NT, preferred_element_type=F32)
            return 0

        lax.fori_loop(0, D // STEP, contract, 0)
        g, u, q = acc[0], acc[1], acc[2]
        sig = jax.nn.sigmoid(g)
        dg_ref[rows, :] = (q * u * sig * (1.0 + g * (1.0 - sig))).astype(BF)
        du_ref[rows, :] = (q * (g * sig)).astype(BF)

    def pair(of):
        def body(i, _):
            hidden(of(i))
            return 0

        lax.fori_loop(0, 2, body, 0)

    def keep(s):
        copy_in(xall.at[rows_of(s), :], x_out.at[rows_of(s), :])

    via_up, via_down = slots_for(), slots_for()
    for t, h in ((0, 0), (0, 1), (1, 0)):
        arrive(to_side[t, h], piece(t, h, side))
        send(via_up[t, h], piece(t, h, side), piece(t, h, side), (ex, up))
        send(via_down[t, h], piece(t, h, side), piece(t, h, side), (ex, down))
    halves = (slice(0, D // 2), slice(D // 2, D))

    def half_piece(s, j):
        return dall.at[pl.ds(pl.multiple_of(s * SHARD + PIECE, PIECE), PIECE), halves[j]]

    far_up, far_down = slot(), slot()
    arrive(to_up[1, 1], piece(1, 1, down))
    send(far_up, half_piece(down, 0), half_piece(down, 0), (ex, up))
    over = [slot(), slot(), slot(), slot()]
    send(over[0], piece(1, 1, down), piece(1, 1, down), (ex, side))
    arrive(to_down[1, 1], piece(1, 1, up))
    send(far_down, half_piece(up, 1), half_piece(up, 1), (ex, down))
    send(over[1], piece(1, 1, up), piece(1, 1, up), (ex, side))
    fwd = {name: slot() for name in ("x0", "x1", "px0", "px1", "d0", "pd0")}
    for t, h in ((0, 0), (0, 1), (1, 0)):
        arrive(to_up[t, h], piece(t, h, down))
        arrive(to_down[t, h], piece(t, h, up))
    send(fwd["x0"], piece(0, 0, down), piece(0, 0, down), (ex, up))
    send(fwd["x1"], piece(0, 1, up), piece(0, 1, up), (ex, down))
    arrive(to_side[1, 1], piece(1, 1, side))
    pair(lambda i: at(i, 0))
    keep(dp)
    keep(side)
    pside_down, pside_up = at(1, NZ - 1), at(1, 1)
    far, pfar = at(0, 2), at(1, 2)
    arrive(via_up[0, 0], piece(0, 0, pside_down))
    send(fwd["px0"], piece(0, 0, pside_down), piece(0, 0, pside_down), (ex, up))
    arrive(via_down[0, 1], piece(0, 1, pside_up))
    send(fwd["px1"], piece(0, 1, pside_up), piece(0, 1, pside_up), (ex, down))
    send(fwd["d0"], piece(1, 0, down), piece(1, 0, down), (ex, up))
    arrive(via_down[1, 0], piece(1, 0, pside_up))
    send(fwd["pd0"], piece(1, 0, pside_up), piece(1, 0, pside_up), (ex, down))
    pair(lambda i: at(0, NZ - 1 - 2 * i))
    keep(down)
    keep(up)
    arrive(far_up, half_piece(far, 0))
    send(over[2], half_piece(far, 0), half_piece(far, 0), (ex, side))
    arrive(far_down, half_piece(far, 1))
    send(over[3], half_piece(far, 1), half_piece(far, 1), (ex, side))
    arrive(via_up[0, 1], piece(0, 1, pside_down))
    arrive(via_up[1, 0], piece(1, 0, pside_down))
    arrive(via_down[0, 0], piece(0, 0, pside_up))
    arrive(over[0], piece(1, 1, pside_down))
    arrive(over[1], piece(1, 1, pside_up))
    pair(lambda i: at(1, NZ - 1 - 2 * i))
    keep(pside_down)
    keep(pside_up)
    arrive(fwd["x0"], piece(0, 0, far))
    arrive(fwd["x1"], piece(0, 1, far))
    arrive(fwd["d0"], piece(1, 0, far))
    arrive(fwd["px0"], piece(0, 0, pfar))
    arrive(fwd["px1"], piece(0, 1, pfar))
    arrive(fwd["pd0"], piece(1, 0, pfar))
    arrive(over[2], half_piece(pfar, 0))
    arrive(over[3], half_piece(pfar, 1))
    pair(lambda i: at(i, 2))
    keep(far)
    keep(pfar)
    for c in sent:
        c.wait_send()
    for c in local[-DP:]:
        c.wait()


def gather_rows(xt, dt, packed, wg, wu, wd):
    hbm = pl.BlockSpec(memory_space=pl.ANY)
    vmem = pl.BlockSpec(memory_space=pltpu.VMEM)
    rows = DP * SHARD
    return pl.pallas_call(
        gather_kernel,
        out_shape=(
            jax.ShapeDtypeStruct((rows, D), BF),
            jax.ShapeDtypeStruct((rows, HID), BF),
            jax.ShapeDtypeStruct((rows, HID), BF),
        ),
        in_specs=[hbm] * 6,
        out_specs=(hbm, vmem, vmem),
        scratch_shapes=[
            pltpu.VMEM((2, WIDE, LOCAL), BF),
            pltpu.VMEM((2 * TOP, LOCAL), BF),
            pltpu.VMEM((CHIPS, LOCAL), F32),
            pltpu.VMEM((CHIPS, LOCAL), F32),
            pltpu.VMEM((CHIPS * PIECE, LOCAL // 2), BF),
            pltpu.VMEM((2, 2, CHIPS, PIECE, WIDE), BF),
            pltpu.VMEM((rows, D), BF),
            pltpu.VMEM((rows, D), BF),
            pltpu.VMEM((D, HID), BF),
            pltpu.VMEM((D, HID), BF),
            pltpu.VMEM((HID, D), BF),
            pltpu.VMEM((3, SHARD, HID), F32),
            pltpu.SemaphoreType.DMA((96,)),
            pltpu.SemaphoreType.DMA((96,)),
            pltpu.SemaphoreType.DMA((24,)),
        ],
        compiler_params=pltpu.CompilerParams(
            collective_id=0, has_side_effects=True, vmem_limit_bytes=60 * 1024 * 1024
        ),
        name="gather_rows",
    )(xt, dt, packed, wg, wu, wd)


def placement(routes, experts, capacity):
    hit = jnp.sum((routes[..., None] == jnp.arange(experts, dtype=routes.dtype)).astype(F32), axis=2)
    tokens = routes.shape[1]
    earlier = (jnp.arange(tokens)[:, None] < jnp.arange(tokens)[None, :]).astype(BF)
    before = jnp.einsum("bse,st->bte", hit.astype(BF), earlier, preferred_element_type=F32)
    at_slot = (before[..., None] == jnp.arange(capacity, dtype=F32)) & (hit[..., None] > 0)
    return jnp.transpose(at_slot, (0, 2, 3, 1)).astype(BF)


def per_device(attn_rows, out_grad, routes, gates, w_gate, w_up, w_down):
    experts = lax.axis_size("expert")
    own = routes.shape[0]
    capacity = 3 * own // 64
    width = attn_rows.shape[1]
    packed = jnp.concatenate([routes.T.astype(BF), gates.T], axis=0)
    gate_mat, up_mat, down_mat = w_gate[0], w_up[0], w_down[0]
    x, dg, du = gather_rows(attn_rows.T, out_grad.T, packed, gate_mat, up_mat, down_mat)

    rows_dims = (((1,), (1,)), ((), ()))
    first_dims = (((0,), (0,)), ((), ()))
    part = lax.dot_general(dg, gate_mat, rows_dims, preferred_element_type=F32)
    part = (part + lax.dot_general(du, up_mat, rows_dims, preferred_element_type=F32)).astype(BF)
    back = lax.psum_scatter(part, "dp", scatter_dimension=0, tiled=True)
    g_gate = lax.dot_general(x, dg, first_dims, preferred_element_type=F32).astype(BF)
    g_up = lax.dot_general(x, du, first_dims, preferred_element_type=F32).astype(BF)
    back = back.reshape(experts * capacity, experts, width)
    back = jnp.transpose(back, (1, 0, 2))
    back = lax.all_to_all(back, "expert", split_axis=0, concat_axis=0, tiled=True)
    back = back.reshape(experts, experts, capacity, width)
    place = placement(lax.all_gather(routes.astype(BF), "expert"), experts, capacity)
    grad_input = jnp.einsum("bect,ebcd->btd", place, back, preferred_element_type=F32).astype(BF)
    return grad_input.reshape(experts * own, width), g_gate[None], g_up[None]


def solution(mesh):
    return jax.shard_map(
        per_device,
        mesh=mesh,
        in_specs=(
            P("dp", "expert"),
            P("dp", "expert"),
            P(("dp", "expert"), None),
            P(("dp", "expert"), None),
            P("expert", None, "dp"),
            P("expert", None, "dp"),
            P("expert", "dp", None),
        ),
        out_specs=(P("dp", "expert"), P("expert", None, "dp"), P("expert", None, "dp")),
        check_vma=False,
    )
```

time: 515 us -> 396 us (0.77)
  waiting for transfers between devices: 328 us -> 96.1 us
  Pallas kernels: 0 us -> 200 us
  blocking collectives: 80.2 us -> 22.7 us
  matrix products: 60.9 us -> 44.4 us
  local copies, waits for them, and re-layouts: 21.8 us -> 8.42 us
    all_gather x2 -> x0, waiting for transfers between devices: 207 us -> none  [dispatch(): return lax.all_gather(got, 'dp', axis=0, tiled=True)]
    pallas_call x0 -> x1, Pallas kernels: none -> 200 us  [gather_rows(): pl.pallas_call(gather_kernel, out_shape=(jax.ShapeDtypeStruct((rows, D),...]
    all_to_all x2 -> x0, blocking collectives: 54.4 us -> none  [dispatch(): lax.all_to_all(sent, 'expert', split_axis=0, concat_axis=0, tiled=True)]
    reduce_scatter x1, waiting for transfers between devices: 117 us -> 82.5 us  [per_device(): back = lax.psum_scatter(part, 'dp', scatter_dimension=0, tiled=True)]
    dot_general x6 -> x1, matrix products: 20.4 us -> 0.14 us  [placement(): jnp.einsum('bse,st->bte', hit.astype(BF), earlier, preferred_element_type...]
    all_to_all x1, waiting for transfers between devices: 4.56 us -> 13.6 us  [per_device(): lax.all_to_all(back, 'expert', split_axis=0, concat_axis=0, tiled=True)]
    reshape x4 -> x0, local copies, waits for them, and re-layouts: 7.1 us -> none  [the longest x2 5.37 us: dispatch(): jnp.transpose(got, (1, 0, 2)).reshape(experts * capacity, experts * width)]
  transfers between devices with their start and end apart: 4 -> 2, of which waited for: 4 -> 2; matrix products, arithmetic and copies ran while one was open for 6% -> 5% of each run, Pallas kernels for 0% -> 0%
where the time goes in v2:
time: 396 us; the launch traced here: 395 us
  Pallas kernels  200 us (51%)
  waiting for transfers between devices  96.1 us (24%)
  matrix products  44.4 us (11%)
  blocking collectives  22.7 us (6%)
  between operations  14.1 us (4%)
  local copies, waits for them, and re-layouts  8.42 us (2%)
  starting transfers between devices  7.1 us (2%)
    pallas_call x1, Pallas kernels, gather_rows(): pl.pallas_call(gather_kernel, out_shape=(jax.ShapeDtypeStruct((rows, D),...  200 us
    reduce_scatter x1, waiting for transfers between devices, per_device(): back = lax.psum_scatter(part, 'dp', scatter_dimension=0, tiled=True)  82.5 us
    all_gather x1, blocking collectives, per_device(): lax.all_gather(routes.astype(BF), 'expert')  22.7 us
    all_to_all x1, waiting for transfers between devices, per_device(): lax.all_to_all(back, 'expert', split_axis=0, concat_axis=0, tiled=True)  13.6 us
    dot_general x1, matrix products, per_device(): part = lax.dot_general(dg, gate_mat, rows_dims, preferred_element_type=F32)  12.7 us
    dot_general x1, matrix products, per_device(): lax.dot_general(du, up_mat, rows_dims, preferred_element_type=F32)  12.6 us
    dot_general x1, matrix products, per_device(): lax.dot_general(x, dg, first_dims, preferred_element_type=F32).astype(BF)  9.19 us
    dot_general x1, matrix products, per_device(): lax.dot_general(x, du, first_dims, preferred_element_type=F32).astype(BF)  9.07 us
  transfers between devices with their start and end apart: 2, of which 2 were waited for; matrix products, arithmetic and copies ran while one was open for 5% of the time, Pallas kernels for 0%

profile of v2, /device:TPU:1, one launch (start us, length us, event | category | flops | bytes accessed | tf_op | source)
XLA Modules:
  0.0 395.3 jit_solution(5471072682281293756)
XLA Ops:
  7.2 0.0 reduce-scatter.2.cloned.1.call-start
  7.2 0.7 convert_bitcast_fusion
  7.9 1.3 pad_maximum_fusion.pk_ref
  9.2 200.4 %gather_rows.1 = (bf16[768,7168]{1,0:T(8,128)(2,1)}, bf16[768,256]{1,0:T(8,128)(2,1)}, bf16[768,256]{1,0:T(8,128)(2,1)}) custom-call(bf16[448,2048]{1,0:T(8,128)(2,1)} %bitcast.48, bf16[448,2048]{1,0:T(8,128)(2,1)} %bitcast.49, bf16[16,128]{1,0:T(8,128)(2,1)} %pad_maximum_fusion.pk_ref, bf16[7168,256]{1,0:T(8,128)(2,1)} %bitcast.44, ...), custom_call_target="tpu_custom_call" | custom-call | tf_op jit(solution)/shard_map/gather_rows/pallas_call | solution.py:281
  209.6 0.0 copy-start
  209.6 0.0 copy-start.1
  209.6 12.7 %fusion.12 = f32[768,7168]{1,0:T(8,128)} fusion(bf16[768,256]{1,0:T(8,128)(2,1)} %get-tuple-element.6, bf16[1,7168,256]{2,1,0:T(8,128)(2,1)} %param.11), kind=kOutput, calls=%fused_computation.21 | convolution fusion | flops 2818572288 | bytes 26083328 | tf_op jit(solution)/shard_map/dot_general | solution.py:334
  222.3 0.0 copy-done
  222.3 0.0 copy-done.1
  222.3 12.6 %add_convert_fusion = bf16[768,7168]{1,0:T(8,128)(2,1)} fusion(f32[768,7168]{1,0:T(8,128)} %fusion.12, bf16[768,256]{1,0:T(8,128)(2,1)S(1)} %copy-done.1, bf16[1,7168,256]{2,1,0:T(8,128)(2,1)S(1)} %copy-done), kind=kOutput, calls=%fused_computation | convolution fusion | flops 2829582336 | bytes 37093376 | tf_op jit(solution)/shard_map/dot_general | solution.py:335
  234.8 0.0 copy-start.3
  234.8 0.0 copy-start.2
  234.9 0.0 reduce-scatter.2.cloned.1.call-update
  234.9 0.7 copy-done.3
  235.5 22.7 %all-gather = bf16[2048,8]{0,1:T(8,128)(2,1)S(1)} all-gather(bf16[128,8]{0,1:T(8,128)(2,1)S(1)} %convert_element_type.27), channel_id=2, replica_groups=mesh['expert'=16,'dp'=8] {'expert'}, dimensions={0}, use_global_device_ids=true | all-gather | bytes 34816 | tf_op jit(solution)/shard_map/all_gather | solution.py:343
  258.2 0.2 convert_reduce_fusion
  258.4 0.1 fusion.7
  258.6 0.0 copy-done.2
  258.6 9.2 %fusion = bf16[1,7168,256]{2,1,0:T(8,128)(2,1)} fusion(bf16[768,7168]{1,0:T(8,128)(2,1)} %get-tuple-element.8, bf16[768,256]{1,0:T(8,128)(2,1)S(1)} %copy-done.2), kind=kOutput, calls=%fused_computation.3 | convolution fusion | flops 2820407296 | bytes 15073280 | tf_op jit(solution)/shard_map/dot_general | solution.py:337
  267.8 82.5 %reduce-scatter.2.cloned.1.call-done = bf16[96,7168]{1,0:T(8,128)(2,1)} async-done(((bf16[768,7168]{1,0:T(8,128)(2,1)}), bf16[96,7168]{1,0:T(8,128)(2,1)}) %reduce-scatter.2.cloned.1.call-update) | async-done | bytes 1376272 | tf_op jit(solution)/shard_map/reduce_scatter | solution.py:336
  350.2 3.1 reshape.21
  353.4 2.0 copy.25
  355.4 7.1 %all-to-all-start = ((bf16[16,96,448]{2,1,0:T(8,128)(2,1)}), bf16[16,96,448]{2,1,0:T(8,128)(2,1)S(1)}, u32[]{:S(2)}, u32[]{:S(2)}) async-start(bf16[16,96,448]{2,1,0:T(8,128)(2,1)} %bitcast.42), calls=%async_computation.1 | async-start | bytes 3145728 | tf_op jit(solution)/shard_map/all_to_all | solution.py:341
  362.4 9.1 %fusion.1 = bf16[1,7168,256]{2,1,0:T(8,128)(2,1)} fusion(bf16[768,7168]{1,0:T(8,128)(2,1)} %get-tuple-element.8, bf16[768,256]{1,0:T(8,128)(2,1)S(1)} %copy-done.1), kind=kOutput, calls=%fused_computation.4 | convolution fusion | flops 2820407296 | bytes 15073280 | tf_op jit(solution)/shard_map/dot_general | solution.py:338
  371.5 13.6 %all-to-all-done = bf16[16,96,448]{2,1,0:T(8,128)(2,1)S(1)} async-done(((bf16[16,96,448]{2,1,0:T(8,128)(2,1)}), bf16[16,96,448]{2,1,0:T(8,128)(2,1)S(1)}, u32[]{:S(2)}, u32[]{:S(2)}) %all-to-all-start) | async-done | bytes 1376288 | tf_op jit(solution)/shard_map/all_to_all | solution.py:341
  385.1 0.9 copy.18
  386.0 0.8 fusion.2
  386.8 1.7 copy.24
  (2 shorter events, 0.0 us)
Async XLA Ops:
  7.2 343.1 %reduce-scatter.2.cloned.1.call-start = ((), (), s32[]{:S(2)}) async-start(), calls=%async_computation.2 | async-start | bytes 12386304 | tf_op jit(solution)/shard_map/reduce_scatter | solution.py:336
  209.6 12.7 %copy-start = (bf16[1,7168,256]{2,1,0:T(8,128)(2,1)S(1)}, bf16[1,7168,256]{2,1,0:T(8,128)(2,1)}, u32[]{:S(2)}) copy-start(bf16[1,7168,256]{2,1,0:T(8,128)(2,1)} %param.12) | copy-start | bytes 11010052
  209.6 12.7 %copy-start.1 = (bf16[768,256]{1,0:T(8,128)(2,1)S(1)}, bf16[768,256]{1,0:T(8,128)(2,1)}, u32[]{:S(2)}) copy-start(bf16[768,256]{1,0:T(8,128)(2,1)} %get-tuple-element.7) | copy-start | bytes 1179652
  234.8 0.7 copy-start.3
  234.8 23.7 %copy-start.2 = (bf16[768,256]{1,0:T(8,128)(2,1)S(1)}, bf16[768,256]{1,0:T(8,128)(2,1)}, u32[]{:S(2)}) copy-start(bf16[768,256]{1,0:T(8,128)(2,1)} %get-tuple-element.6) | copy-start | bytes 1179652
  355.4 29.8 %all-to-all-start = ((bf16[16,96,448]{2,1,0:T(8,128)(2,1)}), bf16[16,96,448]{2,1,0:T(8,128)(2,1)S(1)}, u32[]{:S(2)}, u32[]{:S(2)}) async-start(bf16[16,96,448]{2,1,0:T(8,128)(2,1)} %bitcast.42), calls=%async_computation.1 | async-start | bytes 3145728 | tf_op jit(solution)/shard_map/all_to_all | solution.py:341
Sparse Core Ops, SparseCore 0:
  235.0 115.1 reduce-scatter.1

commit v3 on v2

--- a/solution.py
+++ b/solution.py
@@ -1,5 +1,3 @@
-import functools
-
 import jax
 import jax.numpy as jnp
 from jax import lax
@@ -22,7 +20,7 @@
 
 def gather_kernel(
     xt_ref, dt_ref, pk_ref, wg_ref, wu_ref, wd_ref,
-    x_out, dg_ref, du_ref,
+    x_out, dg_ref, du_ref, tab_out,
     raw, tabs, code, coef, onehot, pay, xall, dall, wg, wu, wd, acc,
     ssem, rsem, lsem,
 ):
@@ -95,6 +93,8 @@
         src = (ex + EXP - r) % EXP
         arrive(tab_slot[r], tabs.at[:, pl.ds(pl.multiple_of(src * TOK, TOK), TOK)])
 
+    copy_in(tabs, tab_out)
+    tab_copy = local[-1]
     table = tabs[...].astype(F32)
     route, gate = table[:TOP], table[TOP:]
     ids = (lax.broadcasted_iota(jnp.int32, (CHIPS, LOCAL), 0) * 2 + core).astype(F32)
@@ -272,6 +272,7 @@
         c.wait_send()
     for c in local[-DP:]:
         c.wait()
+    tab_copy.wait()
 
 
 def gather_rows(xt, dt, packed, wg, wu, wd):
@@ -284,9 +285,10 @@
             jax.ShapeDtypeStruct((rows, D), BF),
             jax.ShapeDtypeStruct((rows, HID), BF),
             jax.ShapeDtypeStruct((rows, HID), BF),
+            jax.ShapeDtypeStruct((2 * TOP, LOCAL), BF),
         ),
         in_specs=[hbm] * 6,
-        out_specs=(hbm, vmem, vmem),
+        out_specs=(hbm, vmem, vmem, hbm),
         scratch_shapes=[
             pltpu.VMEM((2, WIDE, LOCAL), BF),
             pltpu.VMEM((2 * TOP, LOCAL), BF),
@@ -310,39 +312,321 @@
         name="gather_rows",
     )(xt, dt, packed, wg, wu, wd)
 
-
-def placement(routes, experts, capacity):
-    hit = jnp.sum((routes[..., None] == jnp.arange(experts, dtype=routes.dtype)).astype(F32), axis=2)
-    tokens = routes.shape[1]
-    earlier = (jnp.arange(tokens)[:, None] < jnp.arange(tokens)[None, :]).astype(BF)
-    before = jnp.einsum("bse,st->bte", hit.astype(BF), earlier, preferred_element_type=F32)
-    at_slot = (before[..., None] == jnp.arange(capacity, dtype=F32)) & (hit[..., None] > 0)
-    return jnp.transpose(at_slot, (0, 2, 3, 1)).astype(BF)
+NA = 2
+CA = NA * WIDE
+CB = D - CA
+LA, RA = slice(0, CA // 2), slice(CA // 2, CA)
+ALL_A, ALL_B = slice(0, CA), slice(CA, D)
+LB, RB = slice(CA, CA + CB // 2), slice(CA + CB // 2, D)
+PART = 512
+TILE = 512
+
+
+def return_kernel(
+    dg_ref, du_ref, wg_ref, wu_ref, x_ref, tab_ref,
+    out_t, gg_out, gu_out,
+    p, wg, wu, xs, gbuf, tabs, code, onehot, got_a, relay_a, fin_a, relay_b, fin_b, got_b, back, outbuf,
+    ssem, rsem, lsem,
+):
+    ex = lax.axis_index("expert")
+    dp = lax.axis_index("dp")
+    core = ex % 2
+    row, z = dp // NZ, dp % NZ
+
+    def at(y, dz):
+        return y * NZ + (z + dz) % NZ
+
+    up, down, side = at(row, 1), at(row, NZ - 1), at(1 - row, 0)
+
+    barrier = pltpu.get_barrier_semaphore()
+    for r in range(1, EXP):
+        pl.semaphore_signal(barrier, inc=1, device_id=((ex + r) % EXP, dp), device_id_type=MESH)
+    for peer in (up, down, side):
+        pl.semaphore_signal(barrier, inc=1, device_id=(ex, peer), device_id_type=MESH)
+
+    local = []
+
+    def copy(src, dst):
+        c = pltpu.make_async_copy(src, dst, lsem.at[len(local)])
+        c.start()
+        local.append(c)
+        return c
+
+    in_w = [copy(wg_ref, wg), copy(wu_ref, wu)]
+    in_tab = copy(tab_ref, tabs)
+    in_x = copy(x_ref, xs)
+    for c in in_w:
+        c.wait()
+
+    sent = []
+    slots = [0]
+
+    def slot():
+        slots[0] += 1
+        return slots[0] - 1
+
+    def send(k, src, dst, device):
+        c = pltpu.make_async_remote_copy(
+            src_ref=src, dst_ref=dst, send_sem=ssem.at[k], recv_sem=rsem.at[k],
+            device_id=device, device_id_type=MESH,
+        )
+        c.start()
+        sent.append(c)
+
+    def arrive(k, dst):
+        pltpu.make_async_remote_copy(
+            src_ref=dst, dst_ref=dst, send_sem=ssem.at[k], recv_sem=rsem.at[k],
+            device_id=(ex, side), device_id_type=MESH,
+        ).wait_recv()
+
+    def rows_of(s):
+        return pl.ds(pl.multiple_of(s * SHARD, SHARD), SHARD)
+
+    def part_of(s, h):
+        return pl.ds(pl.multiple_of(s * SHARD + h * PIECE, PIECE), PIECE)
+
+    def partial(dz):
+        first, second = rows_of(at(0, dz)), rows_of(at(1, dz))
+        g2 = jnp.concatenate([dg_ref[first, :], dg_ref[second, :]], axis=0)
+        u2 = jnp.concatenate([du_ref[first, :], du_ref[second, :]], axis=0)
+
+        def body(k, _):
+            cols = pl.ds(pl.multiple_of(k * WIDE, WIDE), WIDE)
+            v = lax.dot_general(g2, wg[cols, :], NT, preferred_element_type=F32)
+            v = (v + lax.dot_general(u2, wu[cols, :], NT, preferred_element_type=F32)).astype(BF)
+            p[first, cols] = v[:SHARD]
+            p[second, cols] = v[SHARD:]
+            return 0
+
+        lax.fori_loop(0, D // WIDE, body, 0)
+
+    def add(s, h, cols, *others):
+        def body(i, _):
+            here = pl.ds(pl.multiple_of(s * SHARD + h * PIECE + i * 16, 16), 16)
+            total = p[here, cols].astype(F32)
+            for other in others:
+                total = total + other(pl.ds(pl.multiple_of(h * PIECE + i * 16, 16), 16)).astype(F32)
+            p[here, cols] = total.astype(BF)
+            return 0
+
+        lax.fori_loop(0, PIECE // 16, body, 0)
+
+    half = [slice(h * PIECE, (h + 1) * PIECE) for h in range(2)]
+    s_ya = {(h, dz): slot() for h in range(2) for dz in range(NZ)}
+    s_relay_b = {(h, y, d): slot() for h in range(2) for y in range(2) for d in range(2)}
+    s_fin_l = {(h, y, d): slot() for h in range(2) for y in range(2) for d in range(2)}
+    s_fin_r = {(h, y, d): slot() for h in range(2) for y in range(2) for d in range(2)}
+    s_relay_a = {(h, d): slot() for h in range(2) for d in range(2)}
+    s_fin_a = {(h, d): slot() for h in range(2) for d in range(2)}
+    s_yb = [slot(), slot()]
+    s_back = [[slot() for _ in range(EXP)] for _ in range(2)]
+    rel_l, rel_r = slice(0, CB // 2), slice(CB // 2, CB)
+
+    def over_y(dz, h):
+        send(s_ya[h, dz], p.at[part_of(at(1 - row, dz), h), ALL_A], got_a.at[dz, half[h], :], (ex, side))
+
+    def far_b(h):
+        for y in range(2):
+            src = part_of(at(y, 2), h)
+            send(s_relay_b[h, y, 0], p.at[src, LB], relay_b.at[0, y, half[h], :], (ex, up))
+            send(s_relay_b[h, y, 1], p.at[src, RB], relay_b.at[1, y, half[h], :], (ex, down))
+
+    def direct_up(h):
+        for y in range(2):
+            send(s_fin_r[h, y, 0], p.at[part_of(at(y, 1), h), RB], fin_b.at[0, y, half[h], rel_r], (ex, up))
+
+    def direct_down(h):
+        for y in range(2):
+            send(s_fin_l[h, y, 1], p.at[part_of(at(y, NZ - 1), h), LB], fin_b.at[1, y, half[h], rel_l], (ex, down))
+
+    def combined_b(h):
+        for y in range(2):
+            arrive(s_relay_b[h, y, 0], relay_b.at[0, y, half[h], :])
+            add(at(y, 1), h, LB, lambda r, y=y: relay_b[0, y, r, :])
+            send(s_fin_l[h, y, 0], p.at[part_of(at(y, 1), h), LB], fin_b.at[0, y, half[h], rel_l], (ex, up))
+            arrive(s_relay_b[h, y, 1], relay_b.at[1, y, half[h], :])
+            add(at(y, NZ - 1), h, RB, lambda r, y=y: relay_b[1, y, r, :])
+            send(s_fin_r[h, y, 1], p.at[part_of(at(y, NZ - 1), h), RB], fin_b.at[1, y, half[h], rel_r], (ex, down))
+
+    def far_a(h):
+        arrive(s_ya[h, 2], got_a.at[2, half[h], :])
+        add(at(row, 2), h, ALL_A, lambda r: got_a[2, r, :])
+        src = part_of(at(row, 2), h)
+        send(s_relay_a[h, 0], p.at[src, LA], relay_a.at[0, half[h], :], (ex, up))
+        send(s_relay_a[h, 1], p.at[src, RA], relay_a.at[1, half[h], :], (ex, down))
+
+    def near_a(h):
+        for d, dz, peer, mixed in ((0, 1, up, LA), (1, NZ - 1, down, RA)):
+            arrive(s_ya[h, dz], got_a.at[dz, half[h], :])
+            add(at(row, dz), h, ALL_A, lambda r, dz=dz: got_a[dz, r, :])
+            arrive(s_relay_a[h, d], relay_a.at[d, half[h], :])
+            add(at(row, dz), h, mixed, lambda r, d=d: relay_a[d, r, :])
+            send(s_fin_a[h, d], p.at[part_of(at(row, dz), h), ALL_A], fin_a.at[d, half[h], :], (ex, peer))
+
+    def fold_b(h):
+        for y in range(2):
+            for d in range(2):
+                arrive(s_fin_l[h, y, d], fin_b.at[d, y, half[h], rel_l])
+                arrive(s_fin_r[h, y, d], fin_b.at[d, y, half[h], rel_r])
+        add(side, h, ALL_B, lambda r: fin_b[0, 1 - row, r, :], lambda r: fin_b[1, 1 - row, r, :])
+        send(s_yb[h], p.at[part_of(side, h), ALL_B], got_b.at[half[h], :], (ex, side))
+
+    def finish(h):
+        arrive(s_ya[h, 0], got_a.at[0, half[h], :])
+        for d in range(2):
+            arrive(s_fin_a[h, d], fin_a.at[d, half[h], :])
+        add(dp, h, ALL_A, lambda r: got_a[0, r, :], lambda r: fin_a[0, r, :], lambda r: fin_a[1, r, :])
+        arrive(s_yb[h], got_b.at[half[h], :])
+        add(
+            dp, h, ALL_B,
+            lambda r: fin_b[0, row, r, :], lambda r: fin_b[1, row, r, :], lambda r: got_b[r, :],
+        )
+        where = pl.ds(pl.multiple_of(ex * PIECE, PIECE), PIECE)
+
+        def cols(e):
+            return pl.ds(pl.multiple_of(e // 2 * WIDE + e % 2 * 384, 128), PART)
+
+        for r in range(1, EXP):
+            to = (ex + r) % EXP
+            send(s_back[h][r], p.at[part_of(dp, h), cols(to)], back.at[h, where, :], (to, dp))
+        return copy(p.at[part_of(dp, h), cols(ex)], back.at[h, where, :])
+
+    def combine(h, own):
+        own.wait()
+        for r in range(1, EXP):
+            src = (ex + EXP - r) % EXP
+            arrive(s_back[h][r], back.at[h, pl.ds(pl.multiple_of(src * PIECE, PIECE), PIECE), :])
+        for n in range(0, LOCAL // 2, 256):
+            got = lax.dot_general(
+                back[h], onehot[h, :, n : n + 256], (((0,), (0,)), ((), ())), preferred_element_type=F32
+            )
+            outbuf[:, h * (LOCAL // 2) + n : h * (LOCAL // 2) + n + 256] = got.astype(BF)
+        lanes = slice(h * (LOCAL // 2), (h + 1) * (LOCAL // 2))
+        keep = pl.ds(pl.multiple_of(core * 64, 64), WIDE // 2)
+        return copy(outbuf.at[keep, lanes], out_t.at[:, lanes])
+
+    def place_tables():
+        in_tab.wait()
+        table = tabs[...].astype(F32)[:TOP]
+        ids = lax.broadcasted_iota(jnp.int32, (EXP, LOCAL), 0).astype(F32)
+        hit = jnp.zeros((EXP, LOCAL), F32)
+        for k in range(TOP):
+            hit = hit + jnp.where(table[k : k + 1] == ids, 1.0, 0.0)
+        stacked = jnp.concatenate([hit[:, b * TOK : (b + 1) * TOK] for b in range(EXP)], axis=0)
+        tri = (
+            lax.broadcasted_iota(jnp.int32, (TOK, TOK), 0) < lax.broadcasted_iota(jnp.int32, (TOK, TOK), 1)
+        ).astype(F32).astype(BF)
+        before = jnp.dot(stacked.astype(BF), tri, preferred_element_type=F32)
+        for b in range(EXP):
+            part = slice(b * EXP, (b + 1) * EXP)
+            code[:, b * TOK : (b + 1) * TOK] = jnp.where(
+                stacked[part] > 0.0, before[part] + float(CAP * (b % CHIPS)), -1.0
+            )
+        slot_row = lax.broadcasted_iota(jnp.int32, (PIECE, LOCAL // 2), 0).astype(F32)
+        for h in range(2):
+            for e in range(EXP):
+                equal = code[e : e + 1, h * (LOCAL // 2) : (h + 1) * (LOCAL // 2)] == slot_row
+                onehot[h, e * PIECE : (e + 1) * PIECE] = jnp.where(equal, 1.0, 0.0).astype(BF)
+
+    def weight_grads(start, stop):
+        def body(i, _):
+            cols = pl.ds(pl.multiple_of(i * TILE, TILE), TILE)
+            block = xs[:, cols]
+            dims = (((0,), (0,)), ((), ()))
+            gbuf[0, cols, :] = lax.dot_general(block, dg_ref[...], dims, preferred_element_type=F32).astype(BF)
+            gbuf[1, cols, :] = lax.dot_general(block, du_ref[...], dims, preferred_element_type=F32).astype(BF)
+            return 0
+
+        lax.fori_loop(start, stop, body, 0)
+        span = pl.ds(start * TILE, (stop - start) * TILE)
+        return [copy(gbuf.at[j, span, :], out.at[span, :]) for j, out in enumerate((gg_out, gu_out))]
+
+    partial(2)
+    pl.semaphore_wait(barrier, EXP - 1 + 3)
+    over_y(2, 0)
+    far_b(0)
+    partial(1)
+    over_y(1, 0)
+    direct_up(0)
+    partial(NZ - 1)
+    over_y(NZ - 1, 0)
+    direct_down(0)
+    partial(0)
+    over_y(0, 0)
+    far_a(0)
+    combined_b(0)
+    far_b(1)
+    for dz in (2, 1, NZ - 1, 0):
+        over_y(dz, 1)
+    near_a(0)
+    direct_up(1)
+    direct_down(1)
+    in_x.wait()
+    stores = weight_grads(0, 4)
+    fold_b(0)
+    far_a(1)
+    combined_b(1)
+    place_tables()
+    near_a(1)
+    own0 = finish(0)
+    stores += weight_grads(4, D // TILE)
+    fold_b(1)
+    out0 = combine(0, own0)
+    own1 = finish(1)
+    out1 = combine(1, own1)
+    for c in sent:
+        c.wait_send()
+    for c in stores + [out0, out1]:
+        c.wait()
+
+
+def return_rows(dg, du, wg, wu, x, table):
+    hbm = pl.BlockSpec(memory_space=pl.ANY)
+    vmem = pl.BlockSpec(memory_space=pltpu.VMEM)
+    rows = DP * SHARD
+    return pl.pallas_call(
+        return_kernel,
+        out_shape=(
+            jax.ShapeDtypeStruct((WIDE // 2, LOCAL), BF),
+            jax.ShapeDtypeStruct((D, HID), BF),
+            jax.ShapeDtypeStruct((D, HID), BF),
+        ),
+        in_specs=[vmem, vmem, hbm, hbm, hbm, hbm],
+        out_specs=(hbm, hbm, hbm),
+        scratch_shapes=[
+            pltpu.VMEM((rows, D), BF),
+            pltpu.VMEM((D, HID), BF),
+            pltpu.VMEM((D, HID), BF),
+            pltpu.VMEM((rows, D), BF),
+            pltpu.VMEM((2, D, HID), BF),
+            pltpu.VMEM((2 * TOP, LOCAL), BF),
+            pltpu.VMEM((EXP, LOCAL), F32),
+            pltpu.VMEM((2, EXP * PIECE, LOCAL // 2), BF),
+            pltpu.VMEM((NZ, SHARD, CA), BF),
+            pltpu.VMEM((2, SHARD, CA // 2), BF),
+            pltpu.VMEM((2, SHARD, CA), BF),
+            pltpu.VMEM((2, 2, SHARD, CB // 2), BF),
+            pltpu.VMEM((2, 2, SHARD, CB), BF),
+            pltpu.VMEM((SHARD, CB), BF),
+            pltpu.VMEM((2, EXP * PIECE, PART), BF),
+            pltpu.VMEM((PART, LOCAL), BF),
+            pltpu.SemaphoreType.DMA((100,)),
+            pltpu.SemaphoreType.DMA((100,)),
+            pltpu.SemaphoreType.DMA((16,)),
+        ],
+        compiler_params=pltpu.CompilerParams(
+            collective_id=1, has_side_effects=True, vmem_limit_bytes=63 * 1024 * 1024
+        ),
+        name="return_rows",
+    )(dg, du, wg, wu, x, table)
 
 
 def per_device(attn_rows, out_grad, routes, gates, w_gate, w_up, w_down):
-    experts = lax.axis_size("expert")
-    own = routes.shape[0]
-    capacity = 3 * own // 64
-    width = attn_rows.shape[1]
     packed = jnp.concatenate([routes.T.astype(BF), gates.T], axis=0)
     gate_mat, up_mat, down_mat = w_gate[0], w_up[0], w_down[0]
-    x, dg, du = gather_rows(attn_rows.T, out_grad.T, packed, gate_mat, up_mat, down_mat)
-
-    rows_dims = (((1,), (1,)), ((), ()))
-    first_dims = (((0,), (0,)), ((), ()))
-    part = lax.dot_general(dg, gate_mat, rows_dims, preferred_element_type=F32)
-    part = (part + lax.dot_general(du, up_mat, rows_dims, preferred_element_type=F32)).astype(BF)
-    back = lax.psum_scatter(part, "dp", scatter_dimension=0, tiled=True)
-    g_gate = lax.dot_general(x, dg, first_dims, preferred_element_type=F32).astype(BF)
-    g_up = lax.dot_general(x, du, first_dims, preferred_element_type=F32).astype(BF)
-    back = back.reshape(experts * capacity, experts, width)
-    back = jnp.transpose(back, (1, 0, 2))
-    back = lax.all_to_all(back, "expert", split_axis=0, concat_axis=0, tiled=True)
-    back = back.reshape(experts, experts, capacity, width)
-    place = placement(lax.all_gather(routes.astype(BF), "expert"), experts, capacity)
-    grad_input = jnp.einsum("bect,ebcd->btd", place, back, preferred_element_type=F32).astype(BF)
-    return grad_input.reshape(experts * own, width), g_gate[None], g_up[None]
+    x, dg, du, table = gather_rows(attn_rows.T, out_grad.T, packed, gate_mat, up_mat, down_mat)
+    grad_t, g_gate, g_up = return_rows(dg, du, gate_mat, up_mat, x, table)
+    return grad_t.T, g_gate[None], g_up[None]
 
 
 def solution(mesh):

time: 396 us -> 326 us (0.82)
  Pallas kernels: 200 us -> 315 us
  waiting for transfers between devices: 96.1 us -> 0 us
  matrix products: 44.4 us -> 0 us
  blocking collectives: 22.7 us -> 0 us
  between operations: 14.1 us -> 0.66 us
  starting transfers between devices: 7.1 us -> 0 us
    pallas_call x0 -> x1, Pallas kernels: none -> 114 us  [return_rows(): pl.pallas_call(return_kernel, out_shape=(jax.ShapeDtypeStruct((WIDE // 2,...]
    reduce_scatter x1 -> x0, waiting for transfers between devices: 82.5 us -> none  [per_device(): back = lax.psum_scatter(part, 'dp', scatter_dimension=0, tiled=True)]
    dot_general x6 -> x0, matrix products: 44.4 us -> none  [the longest x1 12.7 us: per_device(): part = lax.dot_general(dg, gate_mat, rows_dims, preferred_element_type=F32)]
    all_gather x1 -> x0, blocking collectives: 22.7 us -> none  [per_device(): lax.all_gather(routes.astype(BF), 'expert')]
    all_to_all x1 -> x0, waiting for transfers between devices: 13.6 us -> none  [per_device(): lax.all_to_all(back, 'expert', split_axis=0, concat_axis=0, tiled=True)]
    unnamed x8 -> x7, local copies, waits for them, and re-layouts: 0.67 us -> 8.29 us
    all_to_all x1 -> x0, starting transfers between devices: 7.06 us -> none  [per_device(): lax.all_to_all(back, 'expert', split_axis=0, concat_axis=0, tiled=True)]
    reshape x3 -> x0, local copies, waits for them, and re-layouts: 6.88 us -> none  [the longest x2 5.13 us: per_device(): back = back.reshape(experts * capacity, experts, width)]
  transfers between devices with their start and end apart: 2 -> 0, of which waited for: 2 -> 0; matrix products, arithmetic and copies ran while one was open for 5% -> 0% of each run, Pallas kernels for 0% -> 0%
where the time goes in v3:
time: 326 us
  Pallas kernels  315 us (97%)
  local copies, waits for them, and re-layouts  8.29 us (3%)
    pallas_call x1, Pallas kernels, gather_rows(): pl.pallas_call(gather_kernel, out_shape=(jax.ShapeDtypeStruct((rows, D),...  201 us
    pallas_call x1, Pallas kernels, return_rows(): pl.pallas_call(return_kernel, out_shape=(jax.ShapeDtypeStruct((WIDE // 2,...  114 us
    unnamed x7, local copies, waits for them, and re-layouts  8.29 us

profile of v3, /device:TPU:1, one launch (start us, length us, event | category | flops | bytes accessed | tf_op | source)
XLA Modules:
  0.0 325.7 jit_solution(12529625420398335881)
XLA Ops:
  0.6 0.7 convert_bitcast_fusion
  1.3 1.3 pad_maximum_fusion.pk_ref
  2.6 200.5 %gather_rows.1 = (bf16[768,7168]{1,0:T(8,128)(2,1)}, bf16[768,256]{1,0:T(8,128)(2,1)}, bf16[768,256]{1,0:T(8,128)(2,1)}, bf16[16,2048]{1,0:T(8,128)(2,1)}) custom-call(bf16[448,2048]{1,0:T(8,128)(2,1)} %bitcast.19, bf16[448,2048]{1,0:T(8,128)(2,1)} %bitcast.20, bf16[16,128]{1,0:T(8,128)(2,1)} %pad_maximum_fusion.pk_ref, bf16[7168,256]{1,0:T(8,128)(2,1)} %bitcast.11, ...), custom_call_target="tpu_custom_call" | custom-call | tf_op jit(solution)/shard_map/gather_rows/pallas_call | solution.py:282
  203.1 114.2 %return_rows.1 = (bf16[448,2048]{1,0:T(8,128)(2,1)}, bf16[7168,256]{1,0:T(8,128)(2,1)}, bf16[7168,256]{1,0:T(8,128)(2,1)}) custom-call(bf16[768,256]{1,0:T(8,128)(2,1)} %get-tuple-element.10.dg_ref, bf16[768,256]{1,0:T(8,128)(2,1)} %get-tuple-element.11.du_ref, bf16[7168,256]{1,0:T(8,128)(2,1)} %bitcast.12, bf16[7168,256]{1,0:T(8,128)(2,1)} %bitcast.14, ...), custom_call_target="tpu_custom_call" | custom-call | tf_op jit(solution)/shard_map/return_rows/pallas_call | solution.py:587
  317.4 0.0 copy-start.1
  317.4 3.1 copy.13
  320.5 0.0 copy-done.1
  320.5 0.0 copy-start
  320.5 1.9 copy.14
  322.3 1.5 copy-done
  323.8 1.8 copy.15
Async XLA Ops:
  317.4 3.1 copy-start.1
  320.5 3.4 %copy-start = (bf16[7168,256]{1,0:T(8,128)(2,1)S(1)}, bf16[7168,256]{1,0:T(8,128)(2,1)}, u32[]{:S(2)}) copy-start(bf16[7168,256]{1,0:T(8,128)(2,1)} %get-tuple-element.16) | copy-start | bytes 11010052

commit v4 on v3

--- a/solution.py
+++ b/solution.py
@@ -143,131 +143,159 @@
             src = (chip + CHIPS - r) % CHIPS
             arrive(a2a_slot[t][h][r], bufs[t].at[own_rows[h], pl.ds(pl.multiple_of(src * WIDE, WIDE), WIDE)])
 
-    def piece(t, h, s):
-        return bufs[t].at[pl.ds(pl.multiple_of(s * SHARD + h * PIECE, PIECE), PIECE), :]
-
-    def slots_for():
-        return {(t, h): slot() for t in range(2) for h in range(2)}
-
-    to_up, to_down, to_side = slots_for(), slots_for(), slots_for()
-
-    def spread(t, h):
-        for k, peer in ((to_side, side), (to_up, up), (to_down, down)):
-            send(k[t, h], piece(t, h, dp), piece(t, h, dp), (ex, peer))
+    def rows_of(s):
+        return pl.ds(pl.multiple_of(s * SHARD, SHARD), SHARD)
+
+    def contract(s, with_x, with_d):
+        rows = rows_of(s)
+        if with_x:
+            acc[0:2] = jnp.zeros((2, SHARD, HID), F32)
+        if with_d:
+            acc[2] = jnp.zeros((SHARD, HID), F32)
+
+        def body(k, _):
+            cols = pl.ds(pl.multiple_of(k * STEP, STEP), STEP)
+            if with_x:
+                xs = xall[rows, cols]
+                acc[0] += jnp.dot(xs, wg[cols, :], preferred_element_type=F32)
+                acc[1] += jnp.dot(xs, wu[cols, :], preferred_element_type=F32)
+            if with_d:
+                acc[2] += lax.dot_general(dall[rows, cols], wd[:, cols], NT, preferred_element_type=F32)
+            return 0
+
+        lax.fori_loop(0, D // STEP, body, 0)
+
+    def activate(s):
+        rows = rows_of(s)
+        g, u, q = acc[0], acc[1], acc[2]
+        sig = jax.nn.sigmoid(g)
+        dg_ref[rows, :] = (q * u * sig * (1.0 + g * (1.0 - sig))).astype(BF)
+        du_ref[rows, :] = (q * (g * sig)).astype(BF)
+        copy_in(xall.at[rows, :], x_out.at[rows, :])
+
+    def hidden(s):
+        contract(s, True, True)
+        activate(s)
+
+    half = D // 2
+    left, right, whole = slice(0, half), slice(half, D), slice(0, D)
+    low, high = slice(0, half // 2), slice(half // 2, half)
+
+    def piece(t, h, s, cols=whole):
+        return bufs[t].at[pl.ds(pl.multiple_of(s * SHARD + h * PIECE, PIECE), PIECE), cols]
+
+    def pass_on(k, to, t, h, s, cols=whole):
+        send(k, piece(t, h, s, cols), piece(t, h, s, cols), (ex, to))
+
+    def slots_for(*names):
+        return {name: slot() for name in names}
+
+    pieces = ((0, 0), (0, 1), (1, 0), (1, 1))
+    to_up, to_down, to_side = slots_for(*pieces), slots_for(*pieces), slots_for(*pieces)
+
+    def spread_z(t, h):
+        pass_on(to_up[t, h], up, t, h, dp)
+        pass_on(to_down[t, h], down, t, h, dp)
+
+    def spread_y(t, h):
+        pass_on(to_side[t, h], side, t, h, dp)
 
     in_raw[0].wait()
     arrive(raw_slot[0], raw.at[0, other, :])
     dispatch(0, 0)
     dispatch(0, 1)
     complete(0, 0)
-    spread(0, 0)
+    spread_z(0, 0)
     in_raw[1].wait()
     arrive(raw_slot[1], raw.at[1, other, :])
     dispatch(1, 0)
     complete(0, 1)
-    spread(0, 1)
+    spread_z(0, 1)
     dispatch(1, 1)
+    spread_y(0, 0)
+    spread_y(0, 1)
     complete(1, 0)
-    spread(1, 0)
+    spread_z(1, 0)
+    spread_y(1, 0)
     complete(1, 1)
-    spread(1, 1)
+    spread_z(1, 1)
+    spread_y(1, 1)
     for c in in_w:
         c.wait()
 
-    def rows_of(s):
-        return pl.ds(pl.multiple_of(s * SHARD, SHARD), SHARD)
-
-    def hidden(s):
-        rows = rows_of(s)
-        acc[...] = jnp.zeros_like(acc)
-
-        def contract(k, _):
-            cols = pl.ds(pl.multiple_of(k * STEP, STEP), STEP)
-            xs = xall[rows, cols]
-            acc[0] += jnp.dot(xs, wg[cols, :], preferred_element_type=F32)
-            acc[1] += jnp.dot(xs, wu[cols, :], preferred_element_type=F32)
-            acc[2] += lax.dot_general(dall[rows, cols], wd[:, cols], NT, preferred_element_type=F32)
-            return 0
-
-        lax.fori_loop(0, D // STEP, contract, 0)
-        g, u, q = acc[0], acc[1], acc[2]
-        sig = jax.nn.sigmoid(g)
-        dg_ref[rows, :] = (q * u * sig * (1.0 + g * (1.0 - sig))).astype(BF)
-        du_ref[rows, :] = (q * (g * sig)).astype(BF)
-
-    def pair(of):
-        def body(i, _):
-            hidden(of(i))
-            return 0
-
-        lax.fori_loop(0, 2, body, 0)
-
-    def keep(s):
-        copy_in(xall.at[rows_of(s), :], x_out.at[rows_of(s), :])
-
-    via_up, via_down = slots_for(), slots_for()
-    for t, h in ((0, 0), (0, 1), (1, 0)):
+    far, pdown, pup, pfar = at(0, 2), at(1, NZ - 1), at(1, 1), at(1, 2)
+    early = ((0, 0, whole), (0, 1, whole), (1, 0, left))
+    via_up, via_down = slots_for(*pieces[:3]), slots_for(*pieces[:3])
+
+    def relay_side(i):
+        t, h, cols = early[i]
         arrive(to_side[t, h], piece(t, h, side))
-        send(via_up[t, h], piece(t, h, side), piece(t, h, side), (ex, up))
-        send(via_down[t, h], piece(t, h, side), piece(t, h, side), (ex, down))
-    halves = (slice(0, D // 2), slice(D // 2, D))
-
-    def half_piece(s, j):
-        return dall.at[pl.ds(pl.multiple_of(s * SHARD + PIECE, PIECE), PIECE), halves[j]]
-
-    far_up, far_down = slot(), slot()
-    arrive(to_up[1, 1], piece(1, 1, down))
-    send(far_up, half_piece(down, 0), half_piece(down, 0), (ex, up))
-    over = [slot(), slot(), slot(), slot()]
-    send(over[0], piece(1, 1, down), piece(1, 1, down), (ex, side))
-    arrive(to_down[1, 1], piece(1, 1, up))
-    send(far_down, half_piece(up, 1), half_piece(up, 1), (ex, down))
-    send(over[1], piece(1, 1, up), piece(1, 1, up), (ex, side))
-    fwd = {name: slot() for name in ("x0", "x1", "px0", "px1", "d0", "pd0")}
-    for t, h in ((0, 0), (0, 1), (1, 0)):
+        pass_on(via_up[t, h], up, t, h, side, cols)
+        pass_on(via_down[t, h], down, t, h, side, cols)
+
+    relay_side(0)
+    hidden(dp)
+    relay_side(1)
+    for t, h in pieces[:2]:
         arrive(to_up[t, h], piece(t, h, down))
         arrive(to_down[t, h], piece(t, h, up))
-    send(fwd["x0"], piece(0, 0, down), piece(0, 0, down), (ex, up))
-    send(fwd["x1"], piece(0, 1, up), piece(0, 1, up), (ex, down))
+    over = slots_for("d", "dr", "u", "ur", "fl", "fr", "f0")
+    two = slots_for("d1l", "d1r", "d0l", "d0r", "x0", "x1", "px0", "px1", "pl", "ph")
+    arrive(to_up[1, 0], piece(1, 0, down))
+    pass_on(over["dr"], side, 1, 0, down, right)
+    arrive(to_down[1, 0], piece(1, 0, up))
+    pass_on(over["ur"], side, 1, 0, up, right)
+    arrive(to_up[1, 1], piece(1, 1, down))
+    pass_on(two["d1l"], up, 1, 1, down, left)
+    pass_on(over["d"], side, 1, 1, down)
+    arrive(to_down[1, 1], piece(1, 1, up))
+    pass_on(two["d1r"], down, 1, 1, up, right)
+    pass_on(over["u"], side, 1, 1, up)
+    pass_on(two["d0l"], up, 1, 0, down, left)
+    pass_on(two["d0r"], down, 1, 0, up, right)
+    relay_side(2)
+    pass_on(two["x0"], up, 0, 0, down)
+    pass_on(two["x1"], down, 0, 1, up)
+    hidden(down)
     arrive(to_side[1, 1], piece(1, 1, side))
-    pair(lambda i: at(i, 0))
-    keep(dp)
-    keep(side)
-    pside_down, pside_up = at(1, NZ - 1), at(1, 1)
-    far, pfar = at(0, 2), at(1, 2)
-    arrive(via_up[0, 0], piece(0, 0, pside_down))
-    send(fwd["px0"], piece(0, 0, pside_down), piece(0, 0, pside_down), (ex, up))
-    arrive(via_down[0, 1], piece(0, 1, pside_up))
-    send(fwd["px1"], piece(0, 1, pside_up), piece(0, 1, pside_up), (ex, down))
-    send(fwd["d0"], piece(1, 0, down), piece(1, 0, down), (ex, up))
-    arrive(via_down[1, 0], piece(1, 0, pside_up))
-    send(fwd["pd0"], piece(1, 0, pside_up), piece(1, 0, pside_up), (ex, down))
-    pair(lambda i: at(0, NZ - 1 - 2 * i))
-    keep(down)
-    keep(up)
-    arrive(far_up, half_piece(far, 0))
-    send(over[2], half_piece(far, 0), half_piece(far, 0), (ex, side))
-    arrive(far_down, half_piece(far, 1))
-    send(over[3], half_piece(far, 1), half_piece(far, 1), (ex, side))
-    arrive(via_up[0, 1], piece(0, 1, pside_down))
-    arrive(via_up[1, 0], piece(1, 0, pside_down))
-    arrive(via_down[0, 0], piece(0, 0, pside_up))
-    arrive(over[0], piece(1, 1, pside_down))
-    arrive(over[1], piece(1, 1, pside_up))
-    pair(lambda i: at(1, NZ - 1 - 2 * i))
-    keep(pside_down)
-    keep(pside_up)
-    arrive(fwd["x0"], piece(0, 0, far))
-    arrive(fwd["x1"], piece(0, 1, far))
-    arrive(fwd["d0"], piece(1, 0, far))
-    arrive(fwd["px0"], piece(0, 0, pfar))
-    arrive(fwd["px1"], piece(0, 1, pfar))
-    arrive(fwd["pd0"], piece(1, 0, pfar))
-    arrive(over[2], half_piece(pfar, 0))
-    arrive(over[3], half_piece(pfar, 1))
-    pair(lambda i: at(i, 2))
-    keep(far)
-    keep(pfar)
+    hidden(side)
+    arrive(via_up[0, 0], piece(0, 0, pdown))
+    pass_on(two["px0"], up, 0, 0, pdown)
+    arrive(via_down[0, 1], piece(0, 1, pup))
+    pass_on(two["px1"], down, 0, 1, pup)
+    hidden(up)
+    arrive(two["d0r"], piece(1, 0, far, right))
+    pass_on(over["f0"], side, 1, 0, far, right)
+    arrive(two["d1l"], piece(1, 1, far, left))
+    pass_on(over["fl"], side, 1, 1, far, left)
+    arrive(two["d1r"], piece(1, 1, far, right))
+    pass_on(over["fr"], side, 1, 1, far, right)
+    arrive(via_up[1, 0], piece(1, 0, pdown, left))
+    pass_on(two["pl"], up, 1, 0, pdown, low)
+    arrive(via_down[1, 0], piece(1, 0, pup, left))
+    pass_on(two["ph"], down, 1, 0, pup, high)
+    arrive(via_up[0, 1], piece(0, 1, pdown))
+    arrive(over["dr"], piece(1, 0, pdown, right))
+    arrive(over["d"], piece(1, 1, pdown))
+    hidden(pdown)
+    arrive(via_down[0, 0], piece(0, 0, pup))
+    arrive(over["ur"], piece(1, 0, pup, right))
+    arrive(over["u"], piece(1, 1, pup))
+    hidden(pup)
+    arrive(two["d0l"], piece(1, 0, far, left))
+    arrive(two["x0"], piece(0, 0, far))
+    arrive(two["x1"], piece(0, 1, far))
+    hidden(far)
+    arrive(over["f0"], piece(1, 0, pfar, right))
+    arrive(over["fl"], piece(1, 1, pfar, left))
+    arrive(over["fr"], piece(1, 1, pfar, right))
+    arrive(two["px0"], piece(0, 0, pfar))
+    arrive(two["px1"], piece(0, 1, pfar))
+    contract(pfar, True, False)
+    arrive(two["pl"], piece(1, 0, pfar, low))
+    arrive(two["ph"], piece(1, 0, pfar, high))
+    contract(pfar, False, True)
+    activate(pfar)
     for c in sent:
         c.wait_send()
     for c in local[-DP:]:
@@ -425,28 +453,31 @@
     def over_y(dz, h):
         send(s_ya[h, dz], p.at[part_of(at(1 - row, dz), h), ALL_A], got_a.at[dz, half[h], :], (ex, side))
 
+    def line(j, dz):
+        return at((row + 1 + j) % 2, dz)
+
     def far_b(h):
         for y in range(2):
-            src = part_of(at(y, 2), h)
+            src = part_of(line(y, 2), h)
             send(s_relay_b[h, y, 0], p.at[src, LB], relay_b.at[0, y, half[h], :], (ex, up))
             send(s_relay_b[h, y, 1], p.at[src, RB], relay_b.at[1, y, half[h], :], (ex, down))
 
     def direct_up(h):
         for y in range(2):
-            send(s_fin_r[h, y, 0], p.at[part_of(at(y, 1), h), RB], fin_b.at[0, y, half[h], rel_r], (ex, up))
+            send(s_fin_r[h, y, 0], p.at[part_of(line(y, 1), h), RB], fin_b.at[0, y, half[h], rel_r], (ex, up))
 
     def direct_down(h):
         for y in range(2):
-            send(s_fin_l[h, y, 1], p.at[part_of(at(y, NZ - 1), h), LB], fin_b.at[1, y, half[h], rel_l], (ex, down))
+            send(s_fin_l[h, y, 1], p.at[part_of(line(y, NZ - 1), h), LB], fin_b.at[1, y, half[h], rel_l], (ex, down))
 
     def combined_b(h):
         for y in range(2):
             arrive(s_relay_b[h, y, 0], relay_b.at[0, y, half[h], :])
-            add(at(y, 1), h, LB, lambda r, y=y: relay_b[0, y, r, :])
-            send(s_fin_l[h, y, 0], p.at[part_of(at(y, 1), h), LB], fin_b.at[0, y, half[h], rel_l], (ex, up))
+            add(line(y, 1), h, LB, lambda r, y=y: relay_b[0, y, r, :])
+            send(s_fin_l[h, y, 0], p.at[part_of(line(y, 1), h), LB], fin_b.at[0, y, half[h], rel_l], (ex, up))
             arrive(s_relay_b[h, y, 1], relay_b.at[1, y, half[h], :])
-            add(at(y, NZ - 1), h, RB, lambda r, y=y: relay_b[1, y, r, :])
-            send(s_fin_r[h, y, 1], p.at[part_of(at(y, NZ - 1), h), RB], fin_b.at[1, y, half[h], rel_r], (ex, down))
+            add(line(y, NZ - 1), h, RB, lambda r, y=y: relay_b[1, y, r, :])
+            send(s_fin_r[h, y, 1], p.at[part_of(line(y, NZ - 1), h), RB], fin_b.at[1, y, half[h], rel_r], (ex, down))
 
     def far_a(h):
         arrive(s_ya[h, 2], got_a.at[2, half[h], :])
@@ -457,18 +488,21 @@
 
     def near_a(h):
         for d, dz, peer, mixed in ((0, 1, up, LA), (1, NZ - 1, down, RA)):
+            plain = RA if d == 0 else LA
             arrive(s_ya[h, dz], got_a.at[dz, half[h], :])
-            add(at(row, dz), h, ALL_A, lambda r, dz=dz: got_a[dz, r, :])
+            add(at(row, dz), h, plain, lambda r, dz=dz: got_a[dz, r, plain])
             arrive(s_relay_a[h, d], relay_a.at[d, half[h], :])
-            add(at(row, dz), h, mixed, lambda r, d=d: relay_a[d, r, :])
+            add(at(row, dz), h, mixed, lambda r, dz=dz: got_a[dz, r, mixed], lambda r, d=d: relay_a[d, r, :])
             send(s_fin_a[h, d], p.at[part_of(at(row, dz), h), ALL_A], fin_a.at[d, half[h], :], (ex, peer))
 
+    def wait_b(h, j):
+        for d in range(2):
+            arrive(s_fin_l[h, j, d], fin_b.at[d, j, half[h], rel_l])
+            arrive(s_fin_r[h, j, d], fin_b.at[d, j, half[h], rel_r])
+
     def fold_b(h):
-        for y in range(2):
-            for d in range(2):
-                arrive(s_fin_l[h, y, d], fin_b.at[d, y, half[h], rel_l])
-                arrive(s_fin_r[h, y, d], fin_b.at[d, y, half[h], rel_r])
-        add(side, h, ALL_B, lambda r: fin_b[0, 1 - row, r, :], lambda r: fin_b[1, 1 - row, r, :])
+        wait_b(h, 0)
+        add(side, h, ALL_B, lambda r: fin_b[0, 0, r, :], lambda r: fin_b[1, 0, r, :])
         send(s_yb[h], p.at[part_of(side, h), ALL_B], got_b.at[half[h], :], (ex, side))
 
     def finish(h):
@@ -476,10 +510,11 @@
         for d in range(2):
             arrive(s_fin_a[h, d], fin_a.at[d, half[h], :])
         add(dp, h, ALL_A, lambda r: got_a[0, r, :], lambda r: fin_a[0, r, :], lambda r: fin_a[1, r, :])
+        wait_b(h, 1)
         arrive(s_yb[h], got_b.at[half[h], :])
         add(
             dp, h, ALL_B,
-            lambda r: fin_b[0, row, r, :], lambda r: fin_b[1, row, r, :], lambda r: got_b[r, :],
+            lambda r: fin_b[0, 1, r, :], lambda r: fin_b[1, 1, r, :], lambda r: got_b[r, :],
         )
         where = pl.ds(pl.multiple_of(ex * PIECE, PIECE), PIECE)
 

time: 326 us -> 302 us (0.926)
  Pallas kernels: 315 us -> 291 us
    pallas_call x1, Pallas kernels: 201 us -> 180 us  [gather_rows(): pl.pallas_call(gather_kernel, out_shape=(jax.ShapeDtypeStruct((rows, D),...]
    pallas_call x1, Pallas kernels: 114 us -> 111 us  [return_rows(): pl.pallas_call(return_kernel, out_shape=(jax.ShapeDtypeStruct((WIDE // 2,...]
where the time goes in v4:
time: 302 us
  Pallas kernels  291 us (96%)
  local copies, waits for them, and re-layouts  8.29 us (3%)
    pallas_call x1, Pallas kernels, gather_rows(): pl.pallas_call(gather_kernel, out_shape=(jax.ShapeDtypeStruct((rows, D),...  180 us
    pallas_call x1, Pallas kernels, return_rows(): pl.pallas_call(return_kernel, out_shape=(jax.ShapeDtypeStruct((WIDE // 2,...  111 us
    unnamed x7, local copies, waits for them, and re-layouts  8.29 us

profile of v4, /device:TPU:1, one launch (start us, length us, event | category | flops | bytes accessed | tf_op | source)
XLA Modules:
  0.0 301.6 jit_solution(444314129229285145)
XLA Ops:
  0.6 0.7 convert_bitcast_fusion
  1.3 1.3 pad_maximum_fusion.pk_ref
  2.6 179.8 %gather_rows.1 = (bf16[768,7168]{1,0:T(8,128)(2,1)}, bf16[768,256]{1,0:T(8,128)(2,1)}, bf16[768,256]{1,0:T(8,128)(2,1)}, bf16[16,2048]{1,0:T(8,128)(2,1)}) custom-call(bf16[448,2048]{1,0:T(8,128)(2,1)} %bitcast.19, bf16[448,2048]{1,0:T(8,128)(2,1)} %bitcast.20, bf16[16,128]{1,0:T(8,128)(2,1)} %pad_maximum_fusion.pk_ref, bf16[7168,256]{1,0:T(8,128)(2,1)} %bitcast.11, ...), custom_call_target="tpu_custom_call" | custom-call | tf_op jit(solution)/shard_map/gather_rows/pallas_call | solution.py:310
  182.4 110.9 %return_rows.1 = (bf16[448,2048]{1,0:T(8,128)(2,1)}, bf16[7168,256]{1,0:T(8,128)(2,1)}, bf16[7168,256]{1,0:T(8,128)(2,1)}) custom-call(bf16[768,256]{1,0:T(8,128)(2,1)} %get-tuple-element.10.dg_ref, bf16[768,256]{1,0:T(8,128)(2,1)} %get-tuple-element.11.du_ref, bf16[7168,256]{1,0:T(8,128)(2,1)} %bitcast.12, bf16[7168,256]{1,0:T(8,128)(2,1)} %bitcast.14, ...), custom_call_target="tpu_custom_call" | custom-call | tf_op jit(solution)/shard_map/return_rows/pallas_call | solution.py:622
  293.3 0.0 copy-start.1
  293.3 3.1 %copy.13 = bf16[2048,448]{0,1:T(8,128)(2,1)} copy(bf16[2048,448]{0,1:T(8,128)(2,1)} %bitcast.18) | data formatting | bytes 3670016
  296.4 0.0 copy-done.1
  296.4 0.0 copy-start
  296.4 1.9 copy.14
  298.3 1.5 copy-done
  299.8 1.8 copy.15
Async XLA Ops:
  293.3 3.1 %copy-start.1 = (bf16[7168,256]{1,0:T(8,128)(2,1)S(1)}, bf16[7168,256]{1,0:T(8,128)(2,1)}, u32[]{:S(2)}) copy-start(bf16[7168,256]{1,0:T(8,128)(2,1)} %get-tuple-element.15) | copy-start | bytes 11010052
  296.4 3.4 %copy-start = (bf16[7168,256]{1,0:T(8,128)(2,1)S(1)}, bf16[7168,256]{1,0:T(8,128)(2,1)}, u32[]{:S(2)}) copy-start(bf16[7168,256]{1,0:T(8,128)(2,1)} %get-tuple-element.16) | copy-start | bytes 11010052

commit v5 on v2

v5 whole, which is shorter than its diff:
```python
import jax
import jax.numpy as jnp
from jax import lax
from jax.experimental import pallas as pl
from jax.experimental.pallas import tpu as pltpu
from jax.sharding import PartitionSpec as P

BF = jnp.bfloat16
F32 = jnp.float32
MESH = pl.DeviceIdType.MESH
NT = (((1,), (1,)), ((), ()))
EXP, DP, NZ, CHIPS = 16, 8, 4, 8
TOK, TOP, CAP = 128, 8, 6
LOCAL = EXP * TOK
WIDE, D, HID = 896, 7168, 256
PIECE = 48
SHARD = 96
STEP = 1024


NA = 2
CA = NA * WIDE
CB = D - CA
LA, RA = slice(0, CA // 2), slice(CA // 2, CA)
ALL_A, ALL_B = slice(0, CA), slice(CA, D)
LB, RB = slice(CA, CA + CB // 2), slice(CA + CB // 2, D)
PART = 512
TILE = 512


def layer_kernel(
    xt_ref, dt_ref, pk_ref, wg_ref, wu_ref, wd_ref,
    out_t, gg_out, gu_out,
    raw, tabs, code, coef, onehot, pay, xall, dall, wg, wu, wd, acc, dg_ref, du_ref,
    spots, places, got_a, relay_a, fin_a, relay_b, fin_b, got_b, back, outbuf, gbuf,
    ssem, rsem, lsem, gsem,
):
    ex = lax.axis_index("expert")
    dp = lax.axis_index("dp")
    core = ex % 2
    chip = ex // 2
    row, z = dp // NZ, dp % NZ

    def at(dy, dz):
        return (row + dy) % 2 * NZ + (z + dz) % NZ

    up, down, side = at(0, 1), at(0, NZ - 1), at(1, 0)
    bufs = (xall, dall)

    barrier = pltpu.get_barrier_semaphore()
    for r in range(1, EXP):
        pl.semaphore_signal(barrier, inc=1, device_id=((ex + r) % EXP, dp), device_id_type=MESH)
    for peer in (up, down, side):
        pl.semaphore_signal(barrier, inc=1, device_id=(ex, peer), device_id_type=MESH)

    local = []

    def copy_in(src, dst):
        c = pltpu.make_async_copy(src, dst, lsem.at[len(local)])
        c.start()
        local.append(c)
        return c

    mine = pl.ds(pl.multiple_of(core * (WIDE // 2), WIDE // 2), WIDE // 2)
    lanes = pl.ds(pl.multiple_of(ex * TOK, TOK), TOK)
    in_tab = copy_in(pk_ref, tabs.at[:, lanes])
    in_raw = [copy_in(ref, raw.at[t, mine, :]) for t, ref in enumerate((xt_ref, dt_ref))]
    in_w = [copy_in(wg_ref, wg), copy_in(wu_ref, wu), copy_in(wd_ref, wd)]

    pl.semaphore_wait(barrier, EXP - 1 + 3)

    sent = {}
    slots = [0]

    def slot():
        slots[0] += 1
        return slots[0] - 1

    def send(k, src, dst, device):
        c = pltpu.make_async_remote_copy(
            src_ref=src, dst_ref=dst, send_sem=ssem.at[k], recv_sem=rsem.at[k],
            device_id=device, device_id_type=MESH,
        )
        c.start()
        sent[k] = c

    def flush(*keys):
        for k in keys:
            sent.pop(k).wait_send()

    def arrive(k, dst):
        pltpu.make_async_remote_copy(
            src_ref=dst, dst_ref=dst, send_sem=ssem.at[k], recv_sem=rsem.at[k],
            device_id=(ex, side), device_id_type=MESH,
        ).wait_recv()

    other = pl.ds(pl.multiple_of((1 - core) * (WIDE // 2), WIDE // 2), WIDE // 2)
    tab_slot = [slot() for _ in range(EXP)]
    for r in range(1, EXP):
        send(tab_slot[r], pk_ref, tabs.at[:, lanes], ((ex + r) % EXP, dp))
    raw_slot = [slot(), slot()]
    sibling = (chip * 2 + 1 - core, dp)
    for t, ref in enumerate((xt_ref, dt_ref)):
        send(raw_slot[t], ref, raw.at[t, mine, :], sibling)

    in_tab.wait()
    for r in range(1, EXP):
        src = (ex + EXP - r) % EXP
        arrive(tab_slot[r], tabs.at[:, pl.ds(pl.multiple_of(src * TOK, TOK), TOK)])

    table = tabs[...].astype(F32)
    route, gate = table[:TOP], table[TOP:]
    ids = (lax.broadcasted_iota(jnp.int32, (CHIPS, LOCAL), 0) * 2 + core).astype(F32)
    hit = jnp.zeros((CHIPS, LOCAL), F32)
    weight = jnp.zeros((CHIPS, LOCAL), F32)
    for k in range(TOP):
        same = route[k : k + 1] == ids
        hit = hit + jnp.where(same, 1.0, 0.0)
        weight = weight + jnp.where(same, gate[k : k + 1], 0.0)
    coef[...] = weight
    stacked = jnp.concatenate([hit[:, b * TOK : (b + 1) * TOK] for b in range(EXP)], axis=0)
    tri = (
        lax.broadcasted_iota(jnp.int32, (TOK, TOK), 0) < lax.broadcasted_iota(jnp.int32, (TOK, TOK), 1)
    ).astype(F32).astype(BF)
    before = jnp.dot(stacked.astype(BF), tri, preferred_element_type=F32)
    for b in range(EXP):
        part = slice(b * CHIPS, (b + 1) * CHIPS)
        code[:, b * TOK : (b + 1) * TOK] = jnp.where(
            stacked[part] > 0.0, before[part] + float(CAP * (b % CHIPS)), -1.0
        )

    slot_row = lax.broadcasted_iota(jnp.int32, (PIECE, LOCAL // 2), 0).astype(F32)
    own_rows = [pl.ds(pl.multiple_of(dp * SHARD + h * PIECE, PIECE), PIECE) for h in range(2)]
    chip_cols = pl.ds(pl.multiple_of(chip * WIDE, WIDE), WIDE)
    a2a_slot = [[[slot() for _ in range(CHIPS)] for _ in range(2)] for _ in range(2)]
    a2a_self = [[None, None], [None, None]]

    def dispatch(t, h):
        half = slice(h * (LOCAL // 2), (h + 1) * (LOCAL // 2))
        for i in range(CHIPS):
            equal = code[i : i + 1, half] == slot_row
            value = 1.0 if t == 0 else coef[i : i + 1, half]
            onehot[i * PIECE : (i + 1) * PIECE] = jnp.where(equal, value, 0.0).astype(BF)
        for n in range(0, WIDE, 128):
            got = lax.dot_general(onehot[...], raw[t, n : n + 128, half], NT, preferred_element_type=F32)
            pay[t, h, :, :, n : n + 128] = got.astype(BF).reshape(CHIPS, PIECE, 128)
        where = bufs[t].at[own_rows[h], chip_cols]
        for r in range(1, CHIPS):
            to = (chip + r) % CHIPS
            send(a2a_slot[t][h][r], pay.at[t, h, to], where, (to * 2 + core, dp))
        a2a_self[t][h] = copy_in(pay.at[t, h, chip], where)

    def complete(t, h):
        a2a_self[t][h].wait()
        for r in range(1, CHIPS):
            src = (chip + CHIPS - r) % CHIPS
            arrive(a2a_slot[t][h][r], bufs[t].at[own_rows[h], pl.ds(pl.multiple_of(src * WIDE, WIDE), WIDE)])

    def rows_of(s):
        return pl.ds(pl.multiple_of(s * SHARD, SHARD), SHARD)

    def contract(s, with_x, with_d):
        rows = rows_of(s)
        if with_x:
            acc[0:2] = jnp.zeros((2, SHARD, HID), F32)
        if with_d:
            acc[2] = jnp.zeros((SHARD, HID), F32)

        def body(k, _):
            cols = pl.ds(pl.multiple_of(k * STEP, STEP), STEP)
            if with_x:
                xs = xall[rows, cols]
                acc[0] += jnp.dot(xs, wg[cols, :], preferred_element_type=F32)
                acc[1] += jnp.dot(xs, wu[cols, :], preferred_element_type=F32)
            if with_d:
                acc[2] += lax.dot_general(dall[rows, cols], wd[:, cols], NT, preferred_element_type=F32)
            return 0

        lax.fori_loop(0, D // STEP, body, 0)

    def activate(s):
        rows = rows_of(s)
        g, u, q = acc[0], acc[1], acc[2]
        sig = jax.nn.sigmoid(g)
        dg_ref[rows, :] = (q * u * sig * (1.0 + g * (1.0 - sig))).astype(BF)
        du_ref[rows, :] = (q * (g * sig)).astype(BF)

    def hidden(s):
        contract(s, True, True)
        activate(s)

    half = D // 2
    left, right, whole = slice(0, half), slice(half, D), slice(0, D)
    low, high = slice(0, half // 2), slice(half // 2, half)

    def piece(t, h, s, cols=whole):
        return bufs[t].at[pl.ds(pl.multiple_of(s * SHARD + h * PIECE, PIECE), PIECE), cols]

    def pass_on(k, to, t, h, s, cols=whole):
        send(k, piece(t, h, s, cols), piece(t, h, s, cols), (ex, to))

    def slots_for(*names):
        return {name: slot() for name in names}

    pieces = ((0, 0), (0, 1), (1, 0), (1, 1))
    to_up, to_down, to_side = slots_for(*pieces), slots_for(*pieces), slots_for(*pieces)

    def spread_z(t, h):
        pass_on(to_up[t, h], up, t, h, dp)
        pass_on(to_down[t, h], down, t, h, dp)

    def spread_y(t, h):
        pass_on(to_side[t, h], side, t, h, dp)

    in_raw[0].wait()
    arrive(raw_slot[0], raw.at[0, other, :])
    dispatch(0, 0)
    dispatch(0, 1)
    complete(0, 0)
    spread_z(0, 0)
    in_raw[1].wait()
    arrive(raw_slot[1], raw.at[1, other, :])
    dispatch(1, 0)
    complete(0, 1)
    spread_z(0, 1)
    dispatch(1, 1)
    spread_y(0, 0)
    spread_y(0, 1)
    complete(1, 0)
    spread_z(1, 0)
    spread_y(1, 0)
    complete(1, 1)
    spread_z(1, 1)
    spread_y(1, 1)
    for c in in_w:
        c.wait()

    far, pdown, pup, pfar = at(0, 2), at(1, NZ - 1), at(1, 1), at(1, 2)
    early = ((0, 0, whole), (0, 1, whole), (1, 0, left))
    via_up, via_down = slots_for(*pieces[:3]), slots_for(*pieces[:3])

    def relay_side(i):
        t, h, cols = early[i]
        arrive(to_side[t, h], piece(t, h, side))
        pass_on(via_up[t, h], up, t, h, side, cols)
        pass_on(via_down[t, h], down, t, h, side, cols)

    relay_side(0)
    hidden(dp)
    relay_side(1)
    for t, h in pieces[:2]:
        arrive(to_up[t, h], piece(t, h, down))
        arrive(to_down[t, h], piece(t, h, up))
    over = slots_for("d", "dr", "u", "ur", "fl", "fr", "f0")
    two = slots_for("d1l", "d1r", "d0l", "d0r", "x0", "x1", "px0", "px1", "pl", "ph")
    arrive(to_up[1, 0], piece(1, 0, down))
    pass_on(over["dr"], side, 1, 0, down, right)
    arrive(to_down[1, 0], piece(1, 0, up))
    pass_on(over["ur"], side, 1, 0, up, right)
    arrive(to_up[1, 1], piece(1, 1, down))
    pass_on(two["d1l"], up, 1, 1, down, left)
    pass_on(over["d"], side, 1, 1, down)
    arrive(to_down[1, 1], piece(1, 1, up))
    pass_on(two["d1r"], down, 1, 1, up, right)
    pass_on(over["u"], side, 1, 1, up)
    pass_on(two["d0l"], up, 1, 0, down, left)
    pass_on(two["d0r"], down, 1, 0, up, right)
    relay_side(2)
    pass_on(two["x0"], up, 0, 0, down)
    pass_on(two["x1"], down, 0, 1, up)
    hidden(down)
    arrive(to_side[1, 1], piece(1, 1, side))
    hidden(side)
    hidden(up)
    arrive(via_up[1, 0], piece(1, 0, pdown, left))
    pass_on(two["pl"], up, 1, 0, pdown, low)
    arrive(via_down[1, 0], piece(1, 0, pup, left))
    pass_on(two["ph"], down, 1, 0, pup, high)
    arrive(via_up[0, 0], piece(0, 0, pdown))
    pass_on(two["px0"], up, 0, 0, pdown)
    arrive(via_down[0, 1], piece(0, 1, pup))
    pass_on(two["px1"], down, 0, 1, pup)
    arrive(two["d0r"], piece(1, 0, far, right))
    pass_on(over["f0"], side, 1, 0, far, right)
    arrive(two["d1l"], piece(1, 1, far, left))
    pass_on(over["fl"], side, 1, 1, far, left)
    arrive(two["d1r"], piece(1, 1, far, right))
    pass_on(over["fr"], side, 1, 1, far, right)
    arrive(via_up[0, 1], piece(0, 1, pdown))
    arrive(over["dr"], piece(1, 0, pdown, right))
    arrive(over["d"], piece(1, 1, pdown))
    hidden(pdown)
    arrive(via_down[0, 0], piece(0, 0, pup))
    arrive(over["ur"], piece(1, 0, pup, right))
    arrive(over["u"], piece(1, 1, pup))
    hidden(pup)
    def part_of(s, h):
        return pl.ds(pl.multiple_of(s * SHARD + h * PIECE, PIECE), PIECE)

    def partial(dz):
        first, second = rows_of(at(0, dz)), rows_of(at(1, dz))
        g2 = jnp.concatenate([dg_ref[first, :], dg_ref[second, :]], axis=0)
        u2 = jnp.concatenate([du_ref[first, :], du_ref[second, :]], axis=0)

        def body(k, _):
            cols = pl.ds(pl.multiple_of(k * WIDE, WIDE), WIDE)
            v = lax.dot_general(g2, wg[cols, :], NT, preferred_element_type=F32)
            v = (v + lax.dot_general(u2, wu[cols, :], NT, preferred_element_type=F32)).astype(BF)
            dall[first, cols] = v[:SHARD]
            dall[second, cols] = v[SHARD:]
            return 0

        lax.fori_loop(0, D // WIDE, body, 0)

    def add(s, h, cols, *others):
        def body(i, _):
            here = pl.ds(pl.multiple_of(s * SHARD + h * PIECE + i * 16, 16), 16)
            total = dall[here, cols].astype(F32)
            for other in others:
                total = total + other(pl.ds(pl.multiple_of(h * PIECE + i * 16, 16), 16)).astype(F32)
            dall[here, cols] = total.astype(BF)
            return 0

        lax.fori_loop(0, PIECE // 16, body, 0)

    rows48 = [slice(h * PIECE, (h + 1) * PIECE) for h in range(2)]
    s_ya = {(h, dz): slot() for h in range(2) for dz in range(NZ)}
    s_relay_b = {(h, y, d): slot() for h in range(2) for y in range(2) for d in range(2)}
    s_fin_l = {(h, y, d): slot() for h in range(2) for y in range(2) for d in range(2)}
    s_fin_r = {(h, y, d): slot() for h in range(2) for y in range(2) for d in range(2)}
    s_relay_a = {(h, d): slot() for h in range(2) for d in range(2)}
    s_fin_a = {(h, d): slot() for h in range(2) for d in range(2)}
    s_yb = [slot(), slot()]
    s_back = [[slot() for _ in range(EXP)] for _ in range(2)]
    rel_l, rel_r = slice(0, CB // 2), slice(CB // 2, CB)

    def over_y(dz, h):
        send(s_ya[h, dz], dall.at[part_of(at(1, dz), h), ALL_A], got_a.at[dz, rows48[h], :], (ex, side))

    def line(j, dz):
        return at(1 - j, dz)

    def far_b(h):
        for y in range(2):
            src = part_of(line(y, 2), h)
            send(s_relay_b[h, y, 0], dall.at[src, LB], relay_b.at[0, y, rows48[h], :], (ex, up))
            send(s_relay_b[h, y, 1], dall.at[src, RB], relay_b.at[1, y, rows48[h], :], (ex, down))

    def direct_up(h):
        for y in range(2):
            send(s_fin_r[h, y, 0], dall.at[part_of(line(y, 1), h), RB], fin_b.at[0, y, rows48[h], rel_r], (ex, up))

    def direct_down(h):
        for y in range(2):
            send(s_fin_l[h, y, 1], dall.at[part_of(line(y, NZ - 1), h), LB], fin_b.at[1, y, rows48[h], rel_l], (ex, down))

    def combined_b(h):
        for y in range(2):
            arrive(s_relay_b[h, y, 0], relay_b.at[0, y, rows48[h], :])
            add(line(y, 1), h, LB, lambda r, y=y: relay_b[0, y, r, :])
            send(s_fin_l[h, y, 0], dall.at[part_of(line(y, 1), h), LB], fin_b.at[0, y, rows48[h], rel_l], (ex, up))
            arrive(s_relay_b[h, y, 1], relay_b.at[1, y, rows48[h], :])
            add(line(y, NZ - 1), h, RB, lambda r, y=y: relay_b[1, y, r, :])
            send(s_fin_r[h, y, 1], dall.at[part_of(line(y, NZ - 1), h), RB], fin_b.at[1, y, rows48[h], rel_r], (ex, down))

    def far_a(h):
        arrive(s_ya[h, 2], got_a.at[2, rows48[h], :])
        add(at(0, 2), h, ALL_A, lambda r: got_a[2, r, :])
        src = part_of(at(0, 2), h)
        send(s_relay_a[h, 0], dall.at[src, LA], relay_a.at[0, rows48[h], :], (ex, up))
        send(s_relay_a[h, 1], dall.at[src, RA], relay_a.at[1, rows48[h], :], (ex, down))

    def near_a(h):
        for d, dz, peer, mixed in ((0, 1, up, LA), (1, NZ - 1, down, RA)):
            plain = RA if d == 0 else LA
            arrive(s_ya[h, dz], got_a.at[dz, rows48[h], :])
            add(at(0, dz), h, plain, lambda r, dz=dz: got_a[dz, r, plain])
            arrive(s_relay_a[h, d], relay_a.at[d, rows48[h], :])
            add(at(0, dz), h, mixed, lambda r, dz=dz: got_a[dz, r, mixed], lambda r, d=d: relay_a[d, r, :])
            send(s_fin_a[h, d], dall.at[part_of(at(0, dz), h), ALL_A], fin_a.at[d, rows48[h], :], (ex, peer))

    def wait_b(h, j):
        for d in range(2):
            arrive(s_fin_l[h, j, d], fin_b.at[d, j, rows48[h], rel_l])
            arrive(s_fin_r[h, j, d], fin_b.at[d, j, rows48[h], rel_r])

    def fold_b(h):
        wait_b(h, 0)
        add(side, h, ALL_B, lambda r: fin_b[0, 0, r, :], lambda r: fin_b[1, 0, r, :])
        send(s_yb[h], dall.at[part_of(side, h), ALL_B], got_b.at[rows48[h], :], (ex, side))

    def finish(h):
        arrive(s_ya[h, 0], got_a.at[0, rows48[h], :])
        for d in range(2):
            arrive(s_fin_a[h, d], fin_a.at[d, rows48[h], :])
        add(dp, h, ALL_A, lambda r: got_a[0, r, :], lambda r: fin_a[0, r, :], lambda r: fin_a[1, r, :])
        wait_b(h, 1)
        arrive(s_yb[h], got_b.at[rows48[h], :])
        add(
            dp, h, ALL_B,
            lambda r: fin_b[0, 1, r, :], lambda r: fin_b[1, 1, r, :], lambda r: got_b[r, :],
        )
        where = pl.ds(pl.multiple_of(ex * PIECE, PIECE), PIECE)

        def cols(e):
            return pl.ds(pl.multiple_of(e // 2 * WIDE + e % 2 * 384, 128), PART)

        for r in range(1, EXP):
            to = (ex + r) % EXP
            send(s_back[h][r], dall.at[part_of(dp, h), cols(to)], back.at[h, where, :], (to, dp))
        return copy_in(dall.at[part_of(dp, h), cols(ex)], back.at[h, where, :])

    def combine(h, own):
        own.wait()
        for r in range(1, EXP):
            src = (ex + EXP - r) % EXP
            arrive(s_back[h][r], back.at[h, pl.ds(pl.multiple_of(src * PIECE, PIECE), PIECE), :])
        for n in range(0, LOCAL // 2, 256):
            got = lax.dot_general(
                back[h], places[h, :, n : n + 256], (((0,), (0,)), ((), ())), preferred_element_type=F32
            )
            outbuf[:, h * (LOCAL // 2) + n : h * (LOCAL // 2) + n + 256] = got.astype(BF)
        lanes = slice(h * (LOCAL // 2), (h + 1) * (LOCAL // 2))
        keep = pl.ds(pl.multiple_of(core * 64, 64), WIDE // 2)
        return copy_in(outbuf.at[keep, lanes], out_t.at[:, lanes])

    def place_tables():
        table = tabs[...].astype(F32)[:TOP]
        ids = lax.broadcasted_iota(jnp.int32, (EXP, LOCAL), 0).astype(F32)
        hit = jnp.zeros((EXP, LOCAL), F32)
        for k in range(TOP):
            hit = hit + jnp.where(table[k : k + 1] == ids, 1.0, 0.0)
        stacked = jnp.concatenate([hit[:, b * TOK : (b + 1) * TOK] for b in range(EXP)], axis=0)
        tri = (
            lax.broadcasted_iota(jnp.int32, (TOK, TOK), 0) < lax.broadcasted_iota(jnp.int32, (TOK, TOK), 1)
        ).astype(F32).astype(BF)
        before = jnp.dot(stacked.astype(BF), tri, preferred_element_type=F32)
        for b in range(EXP):
            part = slice(b * EXP, (b + 1) * EXP)
            spots[:, b * TOK : (b + 1) * TOK] = jnp.where(
                stacked[part] > 0.0, before[part] + float(CAP * (b % CHIPS)), -1.0
            )
        slot_row = lax.broadcasted_iota(jnp.int32, (PIECE, LOCAL // 2), 0).astype(F32)
        for h in range(2):
            for e in range(EXP):
                equal = spots[e : e + 1, h * (LOCAL // 2) : (h + 1) * (LOCAL // 2)] == slot_row
                places[h, e * PIECE : (e + 1) * PIECE] = jnp.where(equal, 1.0, 0.0).astype(BF)

    def grad_copy(j, i):
        cols = pl.ds(pl.multiple_of(i * TILE, TILE), TILE)
        out = gg_out if j == 0 else gu_out
        return pltpu.make_async_copy(gbuf.at[j, i % 2], out.at[cols, :], gsem.at[j, i % 2])

    def weight_grads(start, stop):
        def body(i, _):
            cols = pl.ds(pl.multiple_of(i * TILE, TILE), TILE)
            block = xall[:, cols]
            dims = (((0,), (0,)), ((), ()))
            for j, grad in enumerate((dg_ref, du_ref)):
                @pl.when(i >= 2)
                def _():
                    grad_copy(j, i - 2).wait()

                gbuf[j, i % 2] = lax.dot_general(
                    block, grad[...], dims, preferred_element_type=F32
                ).astype(BF)
                grad_copy(j, i).start()
            return 0

        lax.fori_loop(start, stop, body, 0)

    place_tables()
    flush(*(k[q] for k in (to_up, to_down, to_side) for q in pieces[2:]))
    flush(via_up[1, 0], via_down[1, 0])
    partial(0)
    flush(two["d1r"], two["d0r"], over["u"], over["ur"], two["ph"])
    partial(1)
    direct_up(0)
    flush(two["d1l"], two["d0l"], over["d"], over["dr"], two["pl"])
    partial(NZ - 1)
    direct_down(0)
    arrive(two["d0l"], piece(1, 0, far, left))
    arrive(two["x0"], piece(0, 0, far))
    arrive(two["x1"], piece(0, 1, far))
    hidden(far)
    arrive(two["px0"], piece(0, 0, pfar))
    arrive(two["px1"], piece(0, 1, pfar))
    contract(pfar, True, False)
    arrive(two["pl"], piece(1, 0, pfar, low))
    arrive(two["ph"], piece(1, 0, pfar, high))
    arrive(over["f0"], piece(1, 0, pfar, right))
    arrive(over["fl"], piece(1, 1, pfar, left))
    arrive(over["fr"], piece(1, 1, pfar, right))
    contract(pfar, False, True)
    activate(pfar)
    flush(over["f0"], over["fl"], over["fr"])
    partial(2)
    over_y(2, 0)
    far_b(0)
    for dz in (1, NZ - 1, 0):
        over_y(dz, 0)
    direct_up(1)
    direct_down(1)
    far_a(0)
    far_b(1)
    for dz in (2, 1, NZ - 1, 0):
        over_y(dz, 1)
    combined_b(0)
    near_a(0)
    weight_grads(0, 4)
    far_a(1)
    fold_b(0)
    combined_b(1)
    near_a(1)
    own0 = finish(0)
    weight_grads(4, D // TILE)
    fold_b(1)
    out0 = combine(0, own0)
    own1 = finish(1)
    out1 = combine(1, own1)
    flush(*list(sent))
    for c in (out0, out1):
        c.wait()
    for j in range(2):
        for i in (D // TILE - 2, D // TILE - 1):
            grad_copy(j, i).wait()


def layer(xt, dt, packed, wg, wu, wd):
    hbm = pl.BlockSpec(memory_space=pl.ANY)
    rows = DP * SHARD
    return pl.pallas_call(
        layer_kernel,
        out_shape=(
            jax.ShapeDtypeStruct((WIDE // 2, LOCAL), BF),
            jax.ShapeDtypeStruct((D, HID), BF),
            jax.ShapeDtypeStruct((D, HID), BF),
        ),
        in_specs=[hbm] * 6,
        out_specs=(hbm, hbm, hbm),
        scratch_shapes=[
            pltpu.VMEM((2, WIDE, LOCAL), BF),
            pltpu.VMEM((2 * TOP, LOCAL), BF),
            pltpu.VMEM((CHIPS, LOCAL), F32),
            pltpu.VMEM((CHIPS, LOCAL), F32),
            pltpu.VMEM((CHIPS * PIECE, LOCAL // 2), BF),
            pltpu.VMEM((2, 2, CHIPS, PIECE, WIDE), BF),
            pltpu.VMEM((rows, D), BF),
            pltpu.VMEM((rows, D), BF),
            pltpu.VMEM((D, HID), BF),
            pltpu.VMEM((D, HID), BF),
            pltpu.VMEM((HID, D), BF),
            pltpu.VMEM((3, SHARD, HID), F32),
            pltpu.VMEM((rows, HID), BF),
            pltpu.VMEM((rows, HID), BF),
            pltpu.VMEM((EXP, LOCAL), F32),
            pltpu.VMEM((2, EXP * PIECE, LOCAL // 2), BF),
            pltpu.VMEM((NZ, SHARD, CA), BF),
            pltpu.VMEM((2, SHARD, CA // 2), BF),
            pltpu.VMEM((2, SHARD, CA), BF),
            pltpu.VMEM((2, 2, SHARD, CB // 2), BF),
            pltpu.VMEM((2, 2, SHARD, CB), BF),
            pltpu.VMEM((SHARD, CB), BF),
            pltpu.VMEM((2, EXP * PIECE, PART), BF),
            pltpu.VMEM((PART, LOCAL), BF),
            pltpu.VMEM((2, 2, TILE, HID), BF),
            pltpu.SemaphoreType.DMA((176,)),
            pltpu.SemaphoreType.DMA((176,)),
            pltpu.SemaphoreType.DMA((24,)),
            pltpu.SemaphoreType.DMA((2, 2)),
        ],
        compiler_params=pltpu.CompilerParams(
            collective_id=0, has_side_effects=True, vmem_limit_bytes=67_000_000
        ),
        name="layer",
    )(xt, dt, packed, wg, wu, wd)


def per_device(attn_rows, out_grad, routes, gates, w_gate, w_up, w_down):
    packed = jnp.concatenate([routes.T.astype(BF), gates.T], axis=0)
    grad_t, g_gate, g_up = layer(attn_rows.T, out_grad.T, packed, w_gate[0], w_up[0], w_down[0])
    return grad_t.T, g_gate[None], g_up[None]


def solution(mesh):
    return jax.shard_map(
        per_device,
        mesh=mesh,
        in_specs=(
            P("dp", "expert"),
            P("dp", "expert"),
            P(("dp", "expert"), None),
            P(("dp", "expert"), None),
            P("expert", None, "dp"),
            P("expert", None, "dp"),
            P("expert", "dp", None),
        ),
        out_specs=(P("dp", "expert"), P("expert", None, "dp"), P("expert", None, "dp")),
        check_vma=False,
    )
```

time: 396 us -> 290 us (0.73)
  waiting for transfers between devices: 96.1 us -> 0 us
  Pallas kernels: 200 us -> 277 us
  matrix products: 44.4 us -> 0 us
  blocking collectives: 22.7 us -> 0 us
  between operations: 14.1 us -> 0.65 us
  starting transfers between devices: 7.1 us -> 0 us
    reduce_scatter x1 -> x0, waiting for transfers between devices: 82.5 us -> none  [per_device(): back = lax.psum_scatter(part, 'dp', scatter_dimension=0, tiled=True)]
    pallas_call x1, Pallas kernels: 200 us -> 277 us  [layer(): pl.pallas_call(layer_kernel, out_shape=(jax.ShapeDtypeStruct((WIDE // 2,...]
    dot_general x6 -> x0, matrix products: 44.4 us -> none  [the longest x1 12.7 us: per_device(): part = lax.dot_general(dg, gate_mat, rows_dims, preferred_element_type=F32)]
    all_gather x1 -> x0, blocking collectives: 22.7 us -> none  [per_device(): lax.all_gather(routes.astype(BF), 'expert')]
    all_to_all x1 -> x0, waiting for transfers between devices: 13.6 us -> none  [per_device(): lax.all_to_all(back, 'expert', split_axis=0, concat_axis=0, tiled=True)]
    unnamed x8 -> x7, local copies, waits for them, and re-layouts: 0.67 us -> 8.29 us
    all_to_all x1 -> x0, starting transfers between devices: 7.06 us -> none  [per_device(): lax.all_to_all(back, 'expert', split_axis=0, concat_axis=0, tiled=True)]
    reshape x3 -> x0, local copies, waits for them, and re-layouts: 6.88 us -> none  [the longest x2 5.13 us: per_device(): back = back.reshape(experts * capacity, experts, width)]
  transfers between devices with their start and end apart: 2 -> 0, of which waited for: 2 -> 0; matrix products, arithmetic and copies ran while one was open for 5% -> 0% of each run, Pallas kernels for 0% -> 0%
where the time goes in v5:
time: 290 us; the launch traced here: 288 us
  Pallas kernels  277 us (96%)
  local copies, waits for them, and re-layouts  8.29 us (3%)
    pallas_call x1, Pallas kernels, layer(): pl.pallas_call(layer_kernel, out_shape=(jax.ShapeDtypeStruct((WIDE // 2,...  277 us
    unnamed x7, local copies, waits for them, and re-layouts  8.29 us

profile of v5, /device:TPU:1, one launch (start us, length us, event | category | flops | bytes accessed | tf_op | source)
XLA Modules:
  0.0 288.1 jit_solution(14732539729630738911)
XLA Ops:
  0.6 0.7 convert_bitcast_fusion
  1.3 1.3 pad_maximum_fusion.pk_ref
  2.6 277.2 %layer.1 = (bf16[448,2048]{1,0:T(8,128)(2,1)}, bf16[7168,256]{1,0:T(8,128)(2,1)}, bf16[7168,256]{1,0:T(8,128)(2,1)}) custom-call(bf16[448,2048]{1,0:T(8,128)(2,1)} %bitcast.17, bf16[448,2048]{1,0:T(8,128)(2,1)} %bitcast.18, bf16[16,128]{1,0:T(8,128)(2,1)} %pad_maximum_fusion.pk_ref, bf16[7168,256]{1,0:T(8,128)(2,1)} %bitcast.13, bf16[7168,256]{1,0:T(8,128)(2,1)} %bitcast.14, ...), custom_call_target="tpu_custom_call" | custom-call | tf_op jit(solution)/shard_map/layer/pallas_call | solution.py:532
  279.8 0.0 copy-start.1
  279.8 3.1 %copy.13 = bf16[2048,448]{0,1:T(8,128)(2,1)} copy(bf16[2048,448]{0,1:T(8,128)(2,1)} %bitcast.16) | data formatting | bytes 3670016
  282.9 0.0 copy-done.1
  282.9 0.0 copy-start
  282.9 1.9 copy.14
  284.8 1.5 copy-done
  286.3 1.8 copy.15
Async XLA Ops:
  279.8 3.1 %copy-start.1 = (bf16[7168,256]{1,0:T(8,128)(2,1)S(1)}, bf16[7168,256]{1,0:T(8,128)(2,1)}, u32[]{:S(2)}) copy-start(bf16[7168,256]{1,0:T(8,128)(2,1)} %get-tuple-element.7) | copy-start | bytes 11010052
  282.9 3.4 %copy-start = (bf16[7168,256]{1,0:T(8,128)(2,1)S(1)}, bf16[7168,256]{1,0:T(8,128)(2,1)}, u32[]{:S(2)}) copy-start(bf16[7168,256]{1,0:T(8,128)(2,1)} %get-tuple-element.8) | copy-start | bytes 11010052

commit v6 on v5

--- a/solution.py
+++ b/solution.py
@@ -28,10 +28,18 @@
 TILE = 512
 
 
+def combine(back, places, out, width=256):
+    for n in range(0, LOCAL // 2, width):
+        got = lax.dot_general(
+            back[...], places[:, n : n + width], (((0,), (0,)), ((), ())), preferred_element_type=F32
+        )
+        out[:, n : n + width] = got.astype(BF)
+
+
 def layer_kernel(
-    xt_ref, dt_ref, pk_ref, wg_ref, wu_ref, wd_ref,
-    out_t, gg_out, gu_out,
-    raw, tabs, code, coef, onehot, pay, xall, dall, wg, wu, wd, acc, dg_ref, du_ref,
+    xt_ref, dt_ref, rt_ref, gt_ref, wg_ref, wu_ref, wd_ref,
+    first_out, back_out, place_out, gg_out, gu_out,
+    raw, tab_r, tab_g, code, coef, onehot, pay, xall, dall, wg, wu, wd, acc, dg_ref, du_ref,
     spots, places, got_a, relay_a, fin_a, relay_b, fin_b, got_b, back, outbuf, gbuf,
     ssem, rsem, lsem, gsem,
 ):
@@ -63,7 +71,7 @@
 
     mine = pl.ds(pl.multiple_of(core * (WIDE // 2), WIDE // 2), WIDE // 2)
     lanes = pl.ds(pl.multiple_of(ex * TOK, TOK), TOK)
-    in_tab = copy_in(pk_ref, tabs.at[:, lanes])
+    in_tab = [copy_in(rt_ref, tab_r.at[:, lanes]), copy_in(gt_ref, tab_g.at[:, lanes])]
     in_raw = [copy_in(ref, raw.at[t, mine, :]) for t, ref in enumerate((xt_ref, dt_ref))]
     in_w = [copy_in(wg_ref, wg), copy_in(wu_ref, wu), copy_in(wd_ref, wd)]
 
@@ -95,21 +103,23 @@
         ).wait_recv()
 
     other = pl.ds(pl.multiple_of((1 - core) * (WIDE // 2), WIDE // 2), WIDE // 2)
-    tab_slot = [slot() for _ in range(EXP)]
+    tab_slot = [(slot(), slot()) for _ in range(EXP)]
     for r in range(1, EXP):
-        send(tab_slot[r], pk_ref, tabs.at[:, lanes], ((ex + r) % EXP, dp))
+        send(tab_slot[r][0], rt_ref, tab_r.at[:, lanes], ((ex + r) % EXP, dp))
+        send(tab_slot[r][1], gt_ref, tab_g.at[:, lanes], ((ex + r) % EXP, dp))
     raw_slot = [slot(), slot()]
     sibling = (chip * 2 + 1 - core, dp)
     for t, ref in enumerate((xt_ref, dt_ref)):
         send(raw_slot[t], ref, raw.at[t, mine, :], sibling)
 
-    in_tab.wait()
+    for c in in_tab:
+        c.wait()
     for r in range(1, EXP):
-        src = (ex + EXP - r) % EXP
-        arrive(tab_slot[r], tabs.at[:, pl.ds(pl.multiple_of(src * TOK, TOK), TOK)])
-
-    table = tabs[...].astype(F32)
-    route, gate = table[:TOP], table[TOP:]
+        theirs = pl.ds(pl.multiple_of((ex + EXP - r) % EXP * TOK, TOK), TOK)
+        arrive(tab_slot[r][0], tab_r.at[:, theirs])
+        arrive(tab_slot[r][1], tab_g.at[:, theirs])
+
+    route, gate = tab_r[...].astype(F32), tab_g[...].astype(F32)
     ids = (lax.broadcasted_iota(jnp.int32, (CHIPS, LOCAL), 0) * 2 + core).astype(F32)
     hit = jnp.zeros((CHIPS, LOCAL), F32)
     weight = jnp.zeros((CHIPS, LOCAL), F32)
@@ -209,15 +219,32 @@
         pass_on(to_up[t, h], up, t, h, dp)
         pass_on(to_down[t, h], down, t, h, dp)
 
+    first_up, first_down = [slot() for _ in range(CHIPS)], [slot() for _ in range(CHIPS)]
+    order = (0, 2, 6, 1, 7, 3, 5, 4)
+
+    def chunk(r, s):
+        src = (chip + CHIPS - r) % CHIPS
+        rows = pl.ds(pl.multiple_of(s * SHARD, SHARD), PIECE)
+        return xall.at[rows, pl.ds(pl.multiple_of(src * WIDE, WIDE), WIDE)]
+
+    def spread_first(some):
+        for r in some:
+            if r == 0:
+                a2a_self[0][0].wait()
+            else:
+                arrive(a2a_slot[0][0][r], chunk(r, dp))
+            send(first_up[r], chunk(r, dp), chunk(r, dp), (ex, up))
+            send(first_down[r], chunk(r, dp), chunk(r, dp), (ex, down))
+
     def spread_y(t, h):
         pass_on(to_side[t, h], side, t, h, dp)
 
     in_raw[0].wait()
     arrive(raw_slot[0], raw.at[0, other, :])
     dispatch(0, 0)
+    spread_first(order[:1])
     dispatch(0, 1)
-    complete(0, 0)
-    spread_z(0, 0)
+    spread_first(order[1:])
     in_raw[1].wait()
     arrive(raw_slot[1], raw.at[1, other, :])
     dispatch(1, 0)
@@ -248,9 +275,11 @@
     relay_side(0)
     hidden(dp)
     relay_side(1)
-    for t, h in pieces[:2]:
-        arrive(to_up[t, h], piece(t, h, down))
-        arrive(to_down[t, h], piece(t, h, up))
+    for r in order:
+        arrive(first_up[r], chunk(r, down))
+        arrive(first_down[r], chunk(r, up))
+    arrive(to_up[0, 1], piece(0, 1, down))
+    arrive(to_down[0, 1], piece(0, 1, up))
     over = slots_for("d", "dr", "u", "ur", "fl", "fr", "f0")
     two = slots_for("d1l", "d1r", "d0l", "d0r", "x0", "x1", "px0", "px1", "pl", "ph")
     arrive(to_up[1, 0], piece(1, 0, down))
@@ -389,6 +418,8 @@
         add(side, h, ALL_B, lambda r: fin_b[0, 0, r, :], lambda r: fin_b[1, 0, r, :])
         send(s_yb[h], dall.at[part_of(side, h), ALL_B], got_b.at[rows48[h], :], (ex, side))
 
+    backs = (back, back_out)
+
     def finish(h):
         arrive(s_ya[h, 0], got_a.at[0, rows48[h], :])
         for d in range(2):
@@ -407,25 +438,17 @@
 
         for r in range(1, EXP):
             to = (ex + r) % EXP
-            send(s_back[h][r], dall.at[part_of(dp, h), cols(to)], back.at[h, where, :], (to, dp))
-        return copy_in(dall.at[part_of(dp, h), cols(ex)], back.at[h, where, :])
-
-    def combine(h, own):
+            send(s_back[h][r], dall.at[part_of(dp, h), cols(to)], backs[h].at[where, :], (to, dp))
+        return copy_in(dall.at[part_of(dp, h), cols(ex)], backs[h].at[where, :])
+
+    def returned(h, own):
         own.wait()
         for r in range(1, EXP):
             src = (ex + EXP - r) % EXP
-            arrive(s_back[h][r], back.at[h, pl.ds(pl.multiple_of(src * PIECE, PIECE), PIECE), :])
-        for n in range(0, LOCAL // 2, 256):
-            got = lax.dot_general(
-                back[h], places[h, :, n : n + 256], (((0,), (0,)), ((), ())), preferred_element_type=F32
-            )
-            outbuf[:, h * (LOCAL // 2) + n : h * (LOCAL // 2) + n + 256] = got.astype(BF)
-        lanes = slice(h * (LOCAL // 2), (h + 1) * (LOCAL // 2))
-        keep = pl.ds(pl.multiple_of(core * 64, 64), WIDE // 2)
-        return copy_in(outbuf.at[keep, lanes], out_t.at[:, lanes])
+            arrive(s_back[h][r], backs[h].at[pl.ds(pl.multiple_of(src * PIECE, PIECE), PIECE), :])
 
     def place_tables():
-        table = tabs[...].astype(F32)[:TOP]
+        table = tab_r[...].astype(F32)
         ids = lax.broadcasted_iota(jnp.int32, (EXP, LOCAL), 0).astype(F32)
         hit = jnp.zeros((EXP, LOCAL), F32)
         for k in range(TOP):
@@ -470,6 +493,7 @@
         lax.fori_loop(start, stop, body, 0)
 
     place_tables()
+    place_copy = copy_in(places.at[1], place_out)
     flush(*(k[q] for k in (to_up, to_down, to_side) for q in pieces[2:]))
     flush(via_up[1, 0], via_down[1, 0])
     partial(0)
@@ -515,32 +539,38 @@
     own0 = finish(0)
     weight_grads(4, D // TILE)
     fold_b(1)
-    out0 = combine(0, own0)
     own1 = finish(1)
-    out1 = combine(1, own1)
+    returned(0, own0)
+    combine(back, places.at[0], outbuf)
+    keep = pl.ds(pl.multiple_of(core * 64, 64), WIDE // 2)
+    out0 = copy_in(outbuf.at[keep, :], first_out)
+    returned(1, own1)
     flush(*list(sent))
-    for c in (out0, out1):
-        c.wait()
+    out0.wait()
+    place_copy.wait()
     for j in range(2):
         for i in (D // TILE - 2, D // TILE - 1):
             grad_copy(j, i).wait()
 
 
-def layer(xt, dt, packed, wg, wu, wd):
+def layer(xt, dt, rt, gt, wg, wu, wd):
     hbm = pl.BlockSpec(memory_space=pl.ANY)
     rows = DP * SHARD
     return pl.pallas_call(
         layer_kernel,
         out_shape=(
-            jax.ShapeDtypeStruct((WIDE // 2, LOCAL), BF),
+            jax.ShapeDtypeStruct((WIDE // 2, LOCAL // 2), BF),
+            jax.ShapeDtypeStruct((EXP * PIECE, PART), BF),
+            jax.ShapeDtypeStruct((EXP * PIECE, LOCAL // 2), BF),
             jax.ShapeDtypeStruct((D, HID), BF),
             jax.ShapeDtypeStruct((D, HID), BF),
         ),
-        in_specs=[hbm] * 6,
-        out_specs=(hbm, hbm, hbm),
+        in_specs=[hbm] * 7,
+        out_specs=(hbm,) * 5,
         scratch_shapes=[
             pltpu.VMEM((2, WIDE, LOCAL), BF),
-            pltpu.VMEM((2 * TOP, LOCAL), BF),
+            pltpu.VMEM((TOP, LOCAL), jnp.int32),
+            pltpu.VMEM((TOP, LOCAL), BF),
             pltpu.VMEM((CHIPS, LOCAL), F32),
             pltpu.VMEM((CHIPS, LOCAL), F32),
             pltpu.VMEM((CHIPS * PIECE, LOCAL // 2), BF),
@@ -561,11 +591,11 @@
             pltpu.VMEM((2, 2, SHARD, CB // 2), BF),
             pltpu.VMEM((2, 2, SHARD, CB), BF),
             pltpu.VMEM((SHARD, CB), BF),
-            pltpu.VMEM((2, EXP * PIECE, PART), BF),
-            pltpu.VMEM((PART, LOCAL), BF),
+            pltpu.VMEM((EXP * PIECE, PART), BF),
+            pltpu.VMEM((PART, LOCAL // 2), BF),
             pltpu.VMEM((2, 2, TILE, HID), BF),
-            pltpu.SemaphoreType.DMA((176,)),
-            pltpu.SemaphoreType.DMA((176,)),
+            pltpu.SemaphoreType.DMA((208,)),
+            pltpu.SemaphoreType.DMA((208,)),
             pltpu.SemaphoreType.DMA((24,)),
             pltpu.SemaphoreType.DMA((2, 2)),
         ],
@@ -573,12 +603,88 @@
             collective_id=0, has_side_effects=True, vmem_limit_bytes=67_000_000
         ),
         name="layer",
-    )(xt, dt, packed, wg, wu, wd)
+    )(xt, dt, rt, gt, wg, wu, wd)
+
+
+PARTS = 4
+
+
+def last_kernel(
+    first_ref, back_ref, place_ref, gg_ref, gu_ref,
+    out_t, gg_out, gu_out,
+    first, back, places, out, grads, lsem, gsem, osem,
+):
+    core = lax.axis_index("expert") % 2
+    span = D // PARTS
+    loads = [
+        pltpu.make_async_copy(src, dst, lsem.at[i])
+        for i, (src, dst) in enumerate(((back_ref, back), (place_ref, places), (first_ref, first)))
+    ]
+    pairs = ((gg_ref, gg_out), (gu_ref, gu_out))
+    rows = [slice(n * span, (n + 1) * span) for n in range(PARTS)]
+    takes = [[pltpu.make_async_copy(src.at[r, :], grads.at[j, r, :], gsem.at[0, j, n]) for n, r in enumerate(rows)]
+             for j, (src, _) in enumerate(pairs)]
+    gives = [[pltpu.make_async_copy(grads.at[j, r, :], dst.at[r, :], gsem.at[1, j, n]) for n, r in enumerate(rows)]
+             for j, (_, dst) in enumerate(pairs)]
+    for c in loads:
+        c.start()
+    for n in range(PARTS):
+        for j in range(2):
+            takes[j][n].start()
+    half = LOCAL // 2
+    keep = pl.ds(pl.multiple_of(core * 64, 64), WIDE // 2)
+    for c in loads:
+        c.wait()
+    early = pltpu.make_async_copy(first, out_t.at[:, :half], osem.at[0])
+    late = pltpu.make_async_copy(out.at[keep, :], out_t.at[:, half:], osem.at[1])
+    early.start()
+    width = half // PARTS
+    for n in range(PARTS):
+        cols = slice(n * width, (n + 1) * width)
+        got = lax.dot_general(
+            back[...], places[:, cols], (((0,), (0,)), ((), ())), preferred_element_type=F32
+        )
+        out[:, cols] = got.astype(BF)
+        for j in range(2):
+            takes[j][n].wait()
+            gives[j][n].start()
+    late.start()
+    for n in range(PARTS):
+        for j in range(2):
+            gives[j][n].wait()
+    early.wait()
+    late.wait()
+
+
+def last(first, back, places, gg, gu):
+    hbm = pl.BlockSpec(memory_space=pl.ANY)
+    return pl.pallas_call(
+        last_kernel,
+        out_shape=(
+            jax.ShapeDtypeStruct((WIDE // 2, LOCAL), BF),
+            jax.ShapeDtypeStruct((D, HID), BF),
+            jax.ShapeDtypeStruct((D, HID), BF),
+        ),
+        in_specs=[hbm] * 5,
+        out_specs=(hbm,) * 3,
+        scratch_shapes=[
+            pltpu.VMEM((WIDE // 2, LOCAL // 2), BF),
+            pltpu.VMEM((EXP * PIECE, PART), BF),
+            pltpu.VMEM((EXP * PIECE, LOCAL // 2), BF),
+            pltpu.VMEM((PART, LOCAL // 2), BF),
+            pltpu.VMEM((2, D, HID), BF),
+            pltpu.SemaphoreType.DMA((3,)),
+            pltpu.SemaphoreType.DMA((2, 2, PARTS)),
+            pltpu.SemaphoreType.DMA((2,)),
+        ],
+        compiler_params=pltpu.CompilerParams(vmem_limit_bytes=60 * 1024 * 1024),
+        name="last",
+    )(first, back, places, gg, gu)
 
 
 def per_device(attn_rows, out_grad, routes, gates, w_gate, w_up, w_down):
-    packed = jnp.concatenate([routes.T.astype(BF), gates.T], axis=0)
-    grad_t, g_gate, g_up = layer(attn_rows.T, out_grad.T, packed, w_gate[0], w_up[0], w_down[0])
+    results = layer(attn_rows.T, out_grad.T, routes.T, gates.T, w_gate[0], w_up[0], w_down[0])
+    grad_t, g_gate, g_up = last(*results)
     return grad_t.T, g_gate[None], g_up[None]
 
 

time: 290 us -> 283 us (0.976)
  local copies, waits for them, and re-layouts: 8.29 us -> 0 us
  Pallas kernels: 277 us -> 281 us
    unnamed x7 -> x0, local copies, waits for them, and re-layouts: 8.29 us -> none
    pallas_call x0 -> x1, Pallas kernels: none -> 7.77 us  [last(): pl.pallas_call(last_kernel, out_shape=(jax.ShapeDtypeStruct((WIDE // 2, L...]
    pallas_call x1, Pallas kernels: 277 us -> 273 us  [layer(): pl.pallas_call(layer_kernel, out_shape=(jax.ShapeDtypeStruct((WIDE // 2,...]
where the time goes in v6:
time: 283 us; the launch traced here: 282 us
  Pallas kernels  281 us (99%)
    pallas_call x1, Pallas kernels, layer(): pl.pallas_call(layer_kernel, out_shape=(jax.ShapeDtypeStruct((WIDE // 2,...  273 us
    pallas_call x1, Pallas kernels, last(): pl.pallas_call(last_kernel, out_shape=(jax.ShapeDtypeStruct((WIDE // 2, L...  7.77 us

profile of v6, /device:TPU:1, one launch (start us, length us, event | category | flops | bytes accessed | tf_op | source)
XLA Modules:
  0.0 282.0 jit_solution(278280058425270920)
XLA Ops:
  0.6 273.4 %layer.1 = (bf16[448,1024]{1,0:T(8,128)(2,1)}, bf16[768,512]{1,0:T(8,128)(2,1)}, bf16[768,1024]{1,0:T(8,128)(2,1)}, bf16[7168,256]{1,0:T(8,128)(2,1)}, bf16[7168,256]{1,0:T(8,128)(2,1)}) custom-call(bf16[448,2048]{1,0:T(8,128)(2,1)} %bitcast.13, bf16[448,2048]{1,0:T(8,128)(2,1)} %bitcast.14, s32[8,128]{1,0:T(8,128)} %bitcast.15, bf16[8,128]{1,0:T(8,128)(2,1)} %bitcast.16, ...), custom_call_target="tpu_custom_call" | custom-call | tf_op jit(solution)/shard_map/layer/pallas_call | solution.py:559
  274.1 7.8 %last.1 = (bf16[448,2048]{1,0:T(8,128)(2,1)}, bf16[7168,256]{1,0:T(8,128)(2,1)}, bf16[7168,256]{1,0:T(8,128)(2,1)}) custom-call(bf16[448,1024]{1,0:T(8,128)(2,1)} %get-tuple-element.11.first_ref, bf16[768,512]{1,0:T(8,128)(2,1)} %get-tuple-element.12.back_ref, bf16[768,1024]{1,0:T(8,128)(2,1)} %get-tuple-element.13.place_ref, ...), custom_call_target="tpu_custom_call" | custom-call | tf_op jit(solution)/shard_map/last/pallas_call | solution.py:661

commit v7 on v6

--- a/solution.py
+++ b/solution.py
@@ -369,28 +369,24 @@
     def line(j, dz):
         return at(1 - j, dz)
 
-    def far_b(h):
-        for y in range(2):
-            src = part_of(line(y, 2), h)
-            send(s_relay_b[h, y, 0], dall.at[src, LB], relay_b.at[0, y, rows48[h], :], (ex, up))
-            send(s_relay_b[h, y, 1], dall.at[src, RB], relay_b.at[1, y, rows48[h], :], (ex, down))
-
-    def direct_up(h):
-        for y in range(2):
-            send(s_fin_r[h, y, 0], dall.at[part_of(line(y, 1), h), RB], fin_b.at[0, y, rows48[h], rel_r], (ex, up))
-
-    def direct_down(h):
-        for y in range(2):
-            send(s_fin_l[h, y, 1], dall.at[part_of(line(y, NZ - 1), h), LB], fin_b.at[1, y, rows48[h], rel_l], (ex, down))
-
-    def combined_b(h):
-        for y in range(2):
-            arrive(s_relay_b[h, y, 0], relay_b.at[0, y, rows48[h], :])
-            add(line(y, 1), h, LB, lambda r, y=y: relay_b[0, y, r, :])
-            send(s_fin_l[h, y, 0], dall.at[part_of(line(y, 1), h), LB], fin_b.at[0, y, rows48[h], rel_l], (ex, up))
-            arrive(s_relay_b[h, y, 1], relay_b.at[1, y, rows48[h], :])
-            add(line(y, NZ - 1), h, RB, lambda r, y=y: relay_b[1, y, r, :])
-            send(s_fin_r[h, y, 1], dall.at[part_of(line(y, NZ - 1), h), RB], fin_b.at[1, y, rows48[h], rel_r], (ex, down))
+    def far_b(h, y):
+        src = part_of(line(y, 2), h)
+        send(s_relay_b[h, y, 0], dall.at[src, LB], relay_b.at[0, y, rows48[h], :], (ex, up))
+        send(s_relay_b[h, y, 1], dall.at[src, RB], relay_b.at[1, y, rows48[h], :], (ex, down))
+
+    def direct_up(h, y):
+        send(s_fin_r[h, y, 0], dall.at[part_of(line(y, 1), h), RB], fin_b.at[0, y, rows48[h], rel_r], (ex, up))
+
+    def direct_down(h, y):
+        send(s_fin_l[h, y, 1], dall.at[part_of(line(y, NZ - 1), h), LB], fin_b.at[1, y, rows48[h], rel_l], (ex, down))
+
+    def combined_b(h, y):
+        arrive(s_relay_b[h, y, 0], relay_b.at[0, y, rows48[h], :])
+        add(line(y, 1), h, LB, lambda r, y=y: relay_b[0, y, r, :])
+        send(s_fin_l[h, y, 0], dall.at[part_of(line(y, 1), h), LB], fin_b.at[0, y, rows48[h], rel_l], (ex, up))
+        arrive(s_relay_b[h, y, 1], relay_b.at[1, y, rows48[h], :])
+        add(line(y, NZ - 1), h, RB, lambda r, y=y: relay_b[1, y, r, :])
+        send(s_fin_r[h, y, 1], dall.at[part_of(line(y, NZ - 1), h), RB], fin_b.at[1, y, rows48[h], rel_r], (ex, down))
 
     def far_a(h):
         arrive(s_ya[h, 2], got_a.at[2, rows48[h], :])
@@ -499,10 +495,18 @@
     partial(0)
     flush(two["d1r"], two["d0r"], over["u"], over["ur"], two["ph"])
     partial(1)
-    direct_up(0)
+    for h in range(2):
+        direct_up(h, 0)
     flush(two["d1l"], two["d0l"], over["d"], over["dr"], two["pl"])
     partial(NZ - 1)
-    direct_down(0)
+    for h in range(2):
+        direct_down(h, 0)
+    for h in range(2):
+        direct_up(h, 1)
+        direct_down(h, 1)
+    for dz in (0, 1, NZ - 1):
+        for h in range(2):
+            over_y(dz, h)
     arrive(two["d0l"], piece(1, 0, far, left))
     arrive(two["x0"], piece(0, 0, far))
     arrive(two["x1"], piece(0, 1, far))
@@ -519,26 +523,24 @@
     activate(pfar)
     flush(over["f0"], over["fl"], over["fr"])
     partial(2)
-    over_y(2, 0)
-    far_b(0)
-    for dz in (1, NZ - 1, 0):
-        over_y(dz, 0)
-    direct_up(1)
-    direct_down(1)
+    for y in range(2):
+        for h in range(2):
+            far_b(h, y)
+    for h in range(2):
+        over_y(2, h)
+    weight_grads(0, 6)
+    combined_b(0, 0)
     far_a(0)
-    far_b(1)
-    for dz in (2, 1, NZ - 1, 0):
-        over_y(dz, 1)
-    combined_b(0)
+    far_a(1)
+    combined_b(1, 0)
+    fold_b(0)
     near_a(0)
-    weight_grads(0, 4)
-    far_a(1)
-    fold_b(0)
-    combined_b(1)
     near_a(1)
+    combined_b(0, 1)
+    combined_b(1, 1)
+    fold_b(1)
+    weight_grads(6, D // TILE)
     own0 = finish(0)
-    weight_grads(4, D // TILE)
-    fold_b(1)
     own1 = finish(1)
     returned(0, own0)
     combine(back, places.at[0], outbuf)

time: 283 us -> 273 us (0.965)
  Pallas kernels: 281 us -> 272 us
    pallas_call x1, Pallas kernels: 273 us -> 264 us  [layer(): pl.pallas_call(layer_kernel, out_shape=(jax.ShapeDtypeStruct((WIDE // 2,...]
where the time goes in v7:
time: 273 us
  Pallas kernels  272 us (100%)
    pallas_call x1, Pallas kernels, layer(): pl.pallas_call(layer_kernel, out_shape=(jax.ShapeDtypeStruct((WIDE // 2,...  264 us
    pallas_call x1, Pallas kernels, last(): pl.pallas_call(last_kernel, out_shape=(jax.ShapeDtypeStruct((WIDE // 2, L...  7.77 us

profile of v7, /device:TPU:1, one launch (start us, length us, event | category | flops | bytes accessed | tf_op | source)
XLA Modules:
  0.0 272.6 jit_solution(16005600969944394660)
XLA Ops:
  0.6 264.1 %layer.1 = (bf16[448,1024]{1,0:T(8,128)(2,1)}, bf16[768,512]{1,0:T(8,128)(2,1)}, bf16[768,1024]{1,0:T(8,128)(2,1)}, bf16[7168,256]{1,0:T(8,128)(2,1)}, bf16[7168,256]{1,0:T(8,128)(2,1)}) custom-call(bf16[448,2048]{1,0:T(8,128)(2,1)} %bitcast.13, bf16[448,2048]{1,0:T(8,128)(2,1)} %bitcast.14, s32[8,128]{1,0:T(8,128)} %bitcast.15, bf16[8,128]{1,0:T(8,128)(2,1)} %bitcast.16, ...), custom_call_target="tpu_custom_call" | custom-call | tf_op jit(solution)/shard_map/layer/pallas_call | solution.py:561
  264.7 7.8 %last.1 = (bf16[448,2048]{1,0:T(8,128)(2,1)}, bf16[7168,256]{1,0:T(8,128)(2,1)}, bf16[7168,256]{1,0:T(8,128)(2,1)}) custom-call(bf16[448,1024]{1,0:T(8,128)(2,1)} %get-tuple-element.11.first_ref, bf16[768,512]{1,0:T(8,128)(2,1)} %get-tuple-element.12.back_ref, bf16[768,1024]{1,0:T(8,128)(2,1)} %get-tuple-element.13.place_ref, ...), custom_call_target="tpu_custom_call" | custom-call | tf_op jit(solution)/shard_map/last/pallas_call | solution.py:663

commit v8 on v7

--- a/solution.py
+++ b/solution.py
@@ -73,7 +73,6 @@
     lanes = pl.ds(pl.multiple_of(ex * TOK, TOK), TOK)
     in_tab = [copy_in(rt_ref, tab_r.at[:, lanes]), copy_in(gt_ref, tab_g.at[:, lanes])]
     in_raw = [copy_in(ref, raw.at[t, mine, :]) for t, ref in enumerate((xt_ref, dt_ref))]
-    in_w = [copy_in(wg_ref, wg), copy_in(wu_ref, wu), copy_in(wd_ref, wd)]
 
     pl.semaphore_wait(barrier, EXP - 1 + 3)
 
@@ -245,6 +244,7 @@
     spread_first(order[:1])
     dispatch(0, 1)
     spread_first(order[1:])
+    in_w = [copy_in(wg_ref, wg), copy_in(wu_ref, wu), copy_in(wd_ref, wd)]
     in_raw[1].wait()
     arrive(raw_slot[1], raw.at[1, other, :])
     dispatch(1, 0)
@@ -628,18 +628,18 @@
              for j, (src, _) in enumerate(pairs)]
     gives = [[pltpu.make_async_copy(grads.at[j, r, :], dst.at[r, :], gsem.at[1, j, n]) for n, r in enumerate(rows)]
              for j, (_, dst) in enumerate(pairs)]
-    for c in loads:
+    for c in loads[:2]:
         c.start()
     for n in range(PARTS):
         for j in range(2):
             takes[j][n].start()
+    loads[2].start()
     half = LOCAL // 2
     keep = pl.ds(pl.multiple_of(core * 64, 64), WIDE // 2)
-    for c in loads:
+    for c in loads[:2]:
         c.wait()
     early = pltpu.make_async_copy(first, out_t.at[:, :half], osem.at[0])
     late = pltpu.make_async_copy(out.at[keep, :], out_t.at[:, half:], osem.at[1])
-    early.start()
     width = half // PARTS
     for n in range(PARTS):
         cols = slice(n * width, (n + 1) * width)
@@ -651,6 +651,8 @@
             takes[j][n].wait()
             gives[j][n].start()
     late.start()
+    loads[2].wait()
+    early.start()
     for n in range(PARTS):
         for j in range(2):
             gives[j][n].wait()

time: 273 us -> 273 us (level)
  no operation moved by 1% of the time
where the time goes in v8:
time: 273 us; the launch traced here: 272 us
  Pallas kernels  272 us (100%)
    pallas_call x1, Pallas kernels, layer(): pl.pallas_call(layer_kernel, out_shape=(jax.ShapeDtypeStruct((WIDE // 2,...  264 us
    pallas_call x1, Pallas kernels, last(): pl.pallas_call(last_kernel, out_shape=(jax.ShapeDtypeStruct((WIDE // 2, L...  7.6 us

profile of v8, /device:TPU:1, one launch (start us, length us, event | category | flops | bytes accessed | tf_op | source)
XLA Modules:
  0.0 272.5 jit_solution(11664136786641224761)
XLA Ops:
  0.6 264.1 %layer.1 = (bf16[448,1024]{1,0:T(8,128)(2,1)}, bf16[768,512]{1,0:T(8,128)(2,1)}, bf16[768,1024]{1,0:T(8,128)(2,1)}, bf16[7168,256]{1,0:T(8,128)(2,1)}, bf16[7168,256]{1,0:T(8,128)(2,1)}) custom-call(bf16[448,2048]{1,0:T(8,128)(2,1)} %bitcast.13, bf16[448,2048]{1,0:T(8,128)(2,1)} %bitcast.14, s32[8,128]{1,0:T(8,128)} %bitcast.15, bf16[8,128]{1,0:T(8,128)(2,1)} %bitcast.16, ...), custom_call_target="tpu_custom_call" | custom-call | tf_op jit(solution)/shard_map/layer/pallas_call | solution.py:561
  264.7 7.6 %last.1 = (bf16[448,2048]{1,0:T(8,128)(2,1)}, bf16[7168,256]{1,0:T(8,128)(2,1)}, bf16[7168,256]{1,0:T(8,128)(2,1)}) custom-call(bf16[448,1024]{1,0:T(8,128)(2,1)} %get-tuple-element.11.first_ref, bf16[768,512]{1,0:T(8,128)(2,1)} %get-tuple-element.12.back_ref, bf16[768,1024]{1,0:T(8,128)(2,1)} %get-tuple-element.13.place_ref, ...), custom_call_target="tpu_custom_call" | custom-call | tf_op jit(solution)/shard_map/last/pallas_call | solution.py:665
